TPU v7x, 32 devices: a whole 2x2x4 slice. The times are simulated.
32 devices in a mesh: ctx: 16 (over z, y, x), head: 2 (over core).
Axes of the slice: x: 2, y: 2, z: 4, core: 2. Of those that a mesh axis runs over, the one named last changes fastest.
Arguments:
- queries: bfloat16 [2048, 8192], P('ctx', 'head'), may hold values from -15 to 15
- keys: bfloat16 [2048, 1024], P('ctx', 'head'), may hold values from -6 to 6
- values: bfloat16 [2048, 1024], P('ctx', 'head'), may hold values from -6 to 6
- window: int32 [8], P('head'), may hold values from 512 to 1024, as said below
Outputs:
- loss: float32 [], replicated
- grad_queries: float32 [2048, 8192], P('ctx', 'head')
- grad_keys: float32 [2048, 1024], P('ctx', 'head')
- grad_values: float32 [2048, 1024], P('ctx', 'head')
Inputs may be any that keep to these rules, and one draw needn't show every extreme that they name: Some key-value head's window is exactly 1024.
All inputs are finite; a program needn't handle non-finite values.
Results may differ from a plain program's by a relative error of at most 0.0095.
Values may be sent and summed in bfloat16 or wider, within the bound.
A program may use at most 64 MiB of HBM per device.

v0:
```python
import math

import jax
import jax.numpy as jnp
from jax import lax
from jax.sharding import PartitionSpec as P

QH = 64
KVH = 8
HD = 128
WSPAN = 8


masked_score = -1e30


def passed_along(value, axis, steps):
    count = lax.axis_size(axis)
    first, last = (max(0, -steps), min(count, count - steps))
    return lax.ppermute(value, axis, [(source, source + steps) for source in range(first, last)])


def rounded(values_in):
    return lax.optimization_barrier(values_in.astype(jnp.bfloat16))


def tile_update(softmax_state, query_block, block_keys, block_values, allowed, inverse_root):
    running_max, running_sum, summed = softmax_state
    scores = (
        jnp.einsum("tngd,snd->tngs", query_block, block_keys, preferred_element_type=jnp.float32)
        * inverse_root
    )
    visible = allowed[:, :, None, :]
    scores = jnp.where(visible, scores, masked_score)
    new_max = jnp.maximum(running_max, jnp.max(scores, axis=-1))
    factor = jnp.exp(running_max - new_max)
    weights = jnp.where(visible, jnp.exp(scores - new_max[..., None]), 0.0)
    running_sum = running_sum * factor + jnp.sum(weights, axis=-1)
    summed = summed * factor[..., None] + jnp.einsum(
        "tngs,snd->tngd",
        weights.astype(jnp.bfloat16),
        block_values,
        preferred_element_type=jnp.float32,
    )
    return (new_max, running_sum, summed)


def body(queries, keys, values, window):
    rows_dev = queries.shape[0]
    key_width = keys.shape[1]
    heads_dev = key_width // HD
    group_size = QH // KVH
    cycle_size = lax.axis_size("ctx")
    my_index = lax.axis_index("ctx")
    inverse_root = 1.0 / math.sqrt(HD)
    local_q = queries.reshape(rows_dev, heads_dev, group_size, HD)
    row_ramp = jnp.arange(rows_dev, dtype=jnp.int32)
    query_pos = my_index * rows_dev + row_ramp
    window_base = my_index - WSPAN
    empty_window = jnp.zeros((WSPAN * rows_dev, key_width), jnp.bfloat16)

    def fresh_state(row_count):
        return (
            jnp.full((row_count, heads_dev, group_size), masked_score, jnp.float32),
            jnp.zeros((row_count, heads_dev, group_size), jnp.float32),
            jnp.zeros((row_count, heads_dev, group_size, HD), jnp.float32),
        )

    def causal(key_pos, target_pos):
        visible = key_pos[None, :] <= target_pos[:, None]
        return jnp.broadcast_to(
            visible[:, None, :], (target_pos.shape[0], heads_dev, key_pos.shape[0])
        )

    fold_keys, fold_values = (keys, values)
    initial = ((fresh_state(rows_dev),), empty_window, empty_window)
    piece_keys = lax.all_gather(fold_keys, "ctx", axis=0, tiled=True)
    piece_values = lax.all_gather(fold_values, "ctx", axis=0, tiled=True)
    shard_count = piece_keys.shape[0] // rows_dev

    def visit_shard(offset, folded):
        states, key_window, value_window = folded
        raw_keys = lax.dynamic_slice_in_dim(piece_keys, offset * rows_dev, rows_dev, 0)
        raw_values = lax.dynamic_slice_in_dim(piece_values, offset * rows_dev, rows_dev, 0)
        block_keys = raw_keys.reshape(rows_dev, heads_dev, HD)
        block_values = raw_values.reshape(rows_dev, heads_dev, HD)
        visible = causal(offset * rows_dev + row_ramp, query_pos)
        updated = lax.cond(
            offset <= my_index,
            lambda current: tile_update(
                current, local_q, block_keys, block_values, visible, inverse_root
            ),
            lambda current: current,
            states[0],
        )
        return ((updated,), key_window, value_window)

    folded = lax.fori_loop(0, shard_count, visit_shard, initial)
    finals = [member[2] / member[1][..., None] for member in folded[0]]
    teacher_rows = rounded(finals[0])

    def relay_step(offset, running):
        moving, key_buffer, value_buffer = running
        moving = passed_along(moving, "ctx", 1)
        first_row = (WSPAN - 1 - offset) * rows_dev
        key_buffer = lax.dynamic_update_slice_in_dim(key_buffer, moving[0], first_row, 0)
        value_buffer = lax.dynamic_update_slice_in_dim(value_buffer, moving[1], first_row, 0)
        return (moving, key_buffer, value_buffer)

    relayed = lax.fori_loop(
        0, WSPAN, relay_step, (jnp.stack([keys, values]), empty_window, empty_window)
    )
    key_window, value_window = (relayed[1], relayed[2])
    all_keys = jnp.concatenate([key_window, keys], axis=0).reshape(
        WSPAN + 1, rows_dev, heads_dev, HD
    )
    all_values = jnp.concatenate([value_window, values], axis=0).reshape(
        WSPAN + 1, rows_dev, heads_dev, HD
    )
    shard_ids = window_base + jnp.arange(WSPAN + 1, dtype=jnp.int32)
    widest = jnp.max(window)

    def student_mask(shard):
        key_pos = shard * rows_dev + row_ramp
        below = key_pos[None, None, :] <= query_pos[:, None, None]
        inside = key_pos[None, None, :] > query_pos[:, None, None] - window[None, :, None]
        return below & inside

    def reachable(shard):
        return (shard >= 0) & (shard * rows_dev + rows_dev - 1 > my_index * rows_dev - widest)

    def forward(softmax_state, inputs):
        block_keys, block_values, shard = inputs
        allowed = student_mask(shard)
        updated = lax.cond(
            reachable(shard),
            lambda current: tile_update(
                current, local_q, block_keys, block_values, allowed, inverse_root
            ),
            lambda current: current,
            softmax_state,
        )
        return (updated, shard)

    student_state, visited = lax.scan(
        forward, fresh_state(rows_dev), (all_keys, all_values, shard_ids)
    )
    running_max, running_sum, summed = student_state
    student_out = summed / running_sum[..., None]
    log_total = running_max + jnp.log(running_sum)
    difference = student_out - teacher_rows.astype(jnp.float32)
    square_total = lax.psum(jnp.sum(difference * difference), ("ctx", "head"))
    loss = square_total / (rows_dev * cycle_size * QH * HD)
    grad_out = difference.astype(jnp.bfloat16)
    row_dot = jnp.sum(difference * student_out, axis=-1)

    def backward(grad_query_sum, inputs):
        block_keys, block_values, shard = inputs
        allowed = student_mask(shard)[:, :, None, :]

        def active(current):
            scores = (
                jnp.einsum(
                    "tngd,snd->tngs", local_q, block_keys, preferred_element_type=jnp.float32
                )
                * inverse_root
            )
            scores = jnp.where(allowed, scores, masked_score)
            weights = jnp.where(allowed, jnp.exp(scores - log_total[..., None]), 0.0)
            grad_v = jnp.einsum(
                "tngs,tngd->snd",
                weights.astype(jnp.bfloat16),
                grad_out,
                preferred_element_type=jnp.float32,
            )
            grad_p = jnp.einsum(
                "tngd,snd->tngs", grad_out, block_values, preferred_element_type=jnp.float32
            )
            grad_s = (weights * (grad_p - row_dot[..., None])).astype(jnp.bfloat16)
            current = (
                current
                + jnp.einsum(
                    "tngs,snd->tngd", grad_s, block_keys, preferred_element_type=jnp.float32
                )
                * inverse_root
            )
            grad_k = (
                jnp.einsum("tngs,tngd->snd", grad_s, local_q, preferred_element_type=jnp.float32)
                * inverse_root
            )
            return (current, jnp.stack([grad_k, grad_v]).reshape(2, rows_dev, key_width))

        def skipped(current):
            return (current, jnp.zeros((2, rows_dev, key_width), jnp.float32))

        return lax.cond(reachable(shard), active, skipped, grad_query_sum)

    grad_query_sum, key_terms = lax.scan(
        backward,
        jnp.zeros((rows_dev, heads_dev, group_size, HD), jnp.float32),
        (all_keys, all_values, shard_ids),
    )

    def gather_back(offset, accumulated):
        accumulated = passed_along(accumulated.astype(jnp.bfloat16), "ctx", -1).astype(
            accumulated.dtype
        )
        return accumulated + lax.dynamic_index_in_dim(key_terms, offset, 0, keepdims=False)

    accumulated = lax.fori_loop(1, WSPAN + 1, gather_back, key_terms[0])
    return (loss, grad_query_sum.reshape(rows_dev, -1), accumulated[0], accumulated[1])


def solution(mesh):
    return jax.shard_map(
        body,
        mesh=mesh,
        in_specs=(P("ctx", "head"), P("ctx", "head"), P("ctx", "head"), P("head")),
        out_specs=(P(), P("ctx", "head"), P("ctx", "head"), P("ctx", "head")),
        check_vma=False,
    )
```

profile of v0, /device:TPU:22, one launch (start us, length us, event | category | flops | bytes accessed | tf_op | source)
XLA Modules:
  0.0 480.6 jit_solution(2701854559299171962)
XLA Ops:
  15.0 110.2 %while.89 = (s32[]{:T(128)}, bf16[2,128,512]{2,1,0:T(8,128)(2,1)}, bf16[1024,512]{1,0:T(8,128)(2,1)S(1)}, bf16[1024,512]{1,0:T(8,128)(2,1)}, s32[]{:T(128)}, /*index=5*/s32[]{:T(128)}, s32[]{:T(128)}, s32[]{:T(128)}, s32[]{:T(128)}) while((s32[]{:T(128)}, bf16[2,128,512]{2,1,0:T(8,128)(2,1)}, bf16[1024,512]{1,0:T(8,128)(2,1)S(1)}, ...), condition=%wide.region_1.2_spmd, body=%wide.region_0.1_spmd.sunk | while | flops 7 | bytes 2097355 | solution.py:110
  18.4 8.1 %collective-permute-done = bf16[2,128,512]{2,1,0:T(8,128)(2,1)S(1)} collective-permute-done((bf16[2,128,512]{2,1,0:T(8,128)(2,1)}, bf16[2,128,512]{2,1,0:T(8,128)(2,1)S(1)}, u32[]{:S(2)}, u32[]{:S(2)}) %collective-permute-start) | collective-permute-done | bytes 262176 | tf_op jit(solution)/shard_map/while/body/eval_jaxpr/ppermute | solution.py:20
  27.9 3.9 collective-permute-start
  31.8 5.7 %collective-permute-done = bf16[2,128,512]{2,1,0:T(8,128)(2,1)S(1)} collective-permute-done((bf16[2,128,512]{2,1,0:T(8,128)(2,1)}, bf16[2,128,512]{2,1,0:T(8,128)(2,1)S(1)}, u32[]{:S(2)}, u32[]{:S(2)}) %collective-permute-start) | collective-permute-done | bytes 262176 | tf_op jit(solution)/shard_map/while/body/eval_jaxpr/ppermute | solution.py:20
  38.9 6.4 %collective-permute-start = (bf16[2,128,512]{2,1,0:T(8,128)(2,1)}, bf16[2,128,512]{2,1,0:T(8,128)(2,1)S(1)}, u32[]{:S(2)}, u32[]{:S(2)}) collective-permute-start(bf16[2,128,512]{2,1,0:T(8,128)(2,1)} %get-tuple-element.1881), channel_id=1, source_target_pairs={{0,2},{2,4},{4,6},{6,8},{8,10},{10,12},{12,14},{14,16},{16,18},{18... | collective-permute-start | bytes 786440 | tf_op jit(solution)/shard_map/while/body/eval_jaxpr/ppermute | solution.py:20
  45.3 6.5 %collective-permute-done = bf16[2,128,512]{2,1,0:T(8,128)(2,1)S(1)} collective-permute-done((bf16[2,128,512]{2,1,0:T(8,128)(2,1)}, bf16[2,128,512]{2,1,0:T(8,128)(2,1)S(1)}, u32[]{:S(2)}, u32[]{:S(2)}) %collective-permute-start) | collective-permute-done | bytes 262176 | tf_op jit(solution)/shard_map/while/body/eval_jaxpr/ppermute | solution.py:20
  53.2 6.1 %collective-permute-start = (bf16[2,128,512]{2,1,0:T(8,128)(2,1)}, bf16[2,128,512]{2,1,0:T(8,128)(2,1)S(1)}, u32[]{:S(2)}, u32[]{:S(2)}) collective-permute-start(bf16[2,128,512]{2,1,0:T(8,128)(2,1)} %get-tuple-element.1881), channel_id=1, source_target_pairs={{0,2},{2,4},{4,6},{6,8},{8,10},{10,12},{12,14},{14,16},{16,18},{18... | collective-permute-start | bytes 786440 | tf_op jit(solution)/shard_map/while/body/eval_jaxpr/ppermute | solution.py:20
  59.3 13.1 %collective-permute-done = bf16[2,128,512]{2,1,0:T(8,128)(2,1)S(1)} collective-permute-done((bf16[2,128,512]{2,1,0:T(8,128)(2,1)}, bf16[2,128,512]{2,1,0:T(8,128)(2,1)S(1)}, u32[]{:S(2)}, u32[]{:S(2)}) %collective-permute-start) | collective-permute-done | bytes 262176 | tf_op jit(solution)/shard_map/while/body/eval_jaxpr/ppermute | solution.py:20
  73.8 8.1 %collective-permute-start = (bf16[2,128,512]{2,1,0:T(8,128)(2,1)}, bf16[2,128,512]{2,1,0:T(8,128)(2,1)S(1)}, u32[]{:S(2)}, u32[]{:S(2)}) collective-permute-start(bf16[2,128,512]{2,1,0:T(8,128)(2,1)} %get-tuple-element.1881), channel_id=1, source_target_pairs={{0,2},{2,4},{4,6},{6,8},{8,10},{10,12},{12,14},{14,16},{16,18},{18... | collective-permute-start | bytes 786440 | tf_op jit(solution)/shard_map/while/body/eval_jaxpr/ppermute | solution.py:20
  81.9 4.2 collective-permute-done
  87.4 6.1 %collective-permute-start = (bf16[2,128,512]{2,1,0:T(8,128)(2,1)}, bf16[2,128,512]{2,1,0:T(8,128)(2,1)S(1)}, u32[]{:S(2)}, u32[]{:S(2)}) collective-permute-start(bf16[2,128,512]{2,1,0:T(8,128)(2,1)} %get-tuple-element.1881), channel_id=1, source_target_pairs={{0,2},{2,4},{4,6},{6,8},{8,10},{10,12},{12,14},{14,16},{16,18},{18... | collective-permute-start | bytes 786440 | tf_op jit(solution)/shard_map/while/body/eval_jaxpr/ppermute | solution.py:20
  93.5 4.2 collective-permute-done
  99.0 6.2 %collective-permute-start = (bf16[2,128,512]{2,1,0:T(8,128)(2,1)}, bf16[2,128,512]{2,1,0:T(8,128)(2,1)S(1)}, u32[]{:S(2)}, u32[]{:S(2)}) collective-permute-start(bf16[2,128,512]{2,1,0:T(8,128)(2,1)} %get-tuple-element.1881), channel_id=1, source_target_pairs={{0,2},{2,4},{4,6},{6,8},{8,10},{10,12},{12,14},{14,16},{16,18},{18... | collective-permute-start | bytes 786440 | tf_op jit(solution)/shard_map/while/body/eval_jaxpr/ppermute | solution.py:20
  105.2 4.2 collective-permute-done
  110.8 6.1 %collective-permute-start = (bf16[2,128,512]{2,1,0:T(8,128)(2,1)}, bf16[2,128,512]{2,1,0:T(8,128)(2,1)S(1)}, u32[]{:S(2)}, u32[]{:S(2)}) collective-permute-start(bf16[2,128,512]{2,1,0:T(8,128)(2,1)} %get-tuple-element.1881), channel_id=1, source_target_pairs={{0,2},{2,4},{4,6},{6,8},{8,10},{10,12},{12,14},{14,16},{16,18},{18... | collective-permute-start | bytes 786440 | tf_op jit(solution)/shard_map/while/body/eval_jaxpr/ppermute | solution.py:20
  116.9 6.9 %collective-permute-done = bf16[2,128,512]{2,1,0:T(8,128)(2,1)S(1)} collective-permute-done((bf16[2,128,512]{2,1,0:T(8,128)(2,1)}, bf16[2,128,512]{2,1,0:T(8,128)(2,1)S(1)}, u32[]{:S(2)}, u32[]{:S(2)}) %collective-permute-start) | collective-permute-done | bytes 262176 | tf_op jit(solution)/shard_map/while/body/eval_jaxpr/ppermute | solution.py:20
  134.7 56.8 %while.91 = (s32[]{:T(128)}, f32[128,4,8]{0,2,1:T(8,128)S(1)}, f32[128,4,8]{0,2,1:T(8,128)S(1)}, f32[128,4,8,128]{3,0,2,1:T(8,128)S(1)}, s32[9]{0:T(128)S(1)}, /...) while((s32[]{:T(128)}, f32[128,4,8]{0,2,1:T(8,128)S(1)}, ...), condition=%wide.region_8.9_spmd.clone, body=%wide.region_3.8_spmd.clone.sunk | while | flops 276456192 | bytes 12363651 | solution.py:145
  136.4 4.6 conditional.9
  142.7 4.5 conditional.9
  149.0 4.6 conditional.9
  155.4 4.5 conditional.9
  161.7 4.6 conditional.9
  168.0 4.5 conditional.9
  174.3 4.6 conditional.9
  180.6 4.5 conditional.9
  186.9 4.6 conditional.9
  193.6 45.1 %while.92 = (s32[]{:T(128)}, f32[128,4,8]{0,2,1:T(8,128)S(1)}, f32[128,4,8]{0,2,1:T(8,128)S(1)}, f32[128,4,8,128]{3,0,2,1:T(8,128)S(1)}, s32[]{:T(128)}, /*index...) while((s32[]{:T(128)}, f32[128,4,8]{0,2,1:T(8,128)S(1)}, ...), condition=%wide.region_14.15_spmd.clone, body=%wide.region_9.14_spmd.clone.sunk | while | flops 276324608 | bytes 12652349 | solution.py:98
  244.0 45.9 %psum.7 = f32[]{:T(128)} all-reduce(f32[]{:T(128)} %get-tuple-element.1458), channel_id=1, replica_groups=mesh['ctx'=16,'head'=2] {'ctx','head'}, use_global_device_ids=true, to_apply=%region_16.17 | all-reduce | flops 1 | bytes 8 | tf_op jit(solution)/shard_map/psum | solution.py:152
  290.1 90.2 %while.93 = (s32[]{:T(128)}, f32[128,4,8,128]{3,0,2,1:T(8,128)S(1)}, f32[9,2,128,512]{2,3,1,0:T(8,128)}, s32[9]{0:T(128)S(1)}, s32[]{:T(128)}, /*index=5*/s32[4]...) while((s32[]{:T(128)}, ...), condition=%wide.region_21.22_spmd.clone, body=%wide.region_18.21_spmd.clone.sunk | while | flops 676676352 | bytes 25242512 | solution.py:198
  292.0 7.3 %conditional.11 = (f32[128,4,8,128]{3,0,2,1:T(8,128)S(1)}, f32[1,2,128,512]{2,3,1,0:T(8,128)S(1)}) conditional(s32[]{:T(128)} %convert_element_type.108, f32[128,4,8,128]{3,0,2,1:T(8,128)S(1)} %get-tuple-element.1961, (s32[]{:T(128)}, s32[128]{0:T(128)S(1)}, s32[]{:T(128)}, s32[4]{0:T(128)S(1)}, bf16[9,128,4,128]{3,1,2,0:T(8,128)(2,1)}, ...), branch_computations={%region_19.19_spmd, %region_20.20_spmd} | conditional | flops 676676352 | bytes 24192580 | solution.py:196
  302.1 7.3 %conditional.11 = (f32[128,4,8,128]{3,0,2,1:T(8,128)S(1)}, f32[1,2,128,512]{2,3,1,0:T(8,128)S(1)}) conditional(s32[]{:T(128)} %convert_element_type.108, f32[128,4,8,128]{3,0,2,1:T(8,128)S(1)} %get-tuple-element.1961, (s32[]{:T(128)}, s32[128]{0:T(128)S(1)}, s32[]{:T(128)}, s32[4]{0:T(128)S(1)}, bf16[9,128,4,128]{3,1,2,0:T(8,128)(2,1)}, ...), branch_computations={%region_19.19_spmd, %region_20.20_spmd} | conditional | flops 676676352 | bytes 24192580 | solution.py:196
  312.1 7.3 %conditional.11 = (f32[128,4,8,128]{3,0,2,1:T(8,128)S(1)}, f32[1,2,128,512]{2,3,1,0:T(8,128)S(1)}) conditional(s32[]{:T(128)} %convert_element_type.108, f32[128,4,8,128]{3,0,2,1:T(8,128)S(1)} %get-tuple-element.1961, (s32[]{:T(128)}, s32[128]{0:T(128)S(1)}, s32[]{:T(128)}, s32[4]{0:T(128)S(1)}, bf16[9,128,4,128]{3,1,2,0:T(8,128)(2,1)}, ...), branch_computations={%region_19.19_spmd, %region_20.20_spmd} | conditional | flops 676676352 | bytes 24192580 | solution.py:196
  322.1 7.3 %conditional.11 = (f32[128,4,8,128]{3,0,2,1:T(8,128)S(1)}, f32[1,2,128,512]{2,3,1,0:T(8,128)S(1)}) conditional(s32[]{:T(128)} %convert_element_type.108, f32[128,4,8,128]{3,0,2,1:T(8,128)S(1)} %get-tuple-element.1961, (s32[]{:T(128)}, s32[128]{0:T(128)S(1)}, s32[]{:T(128)}, s32[4]{0:T(128)S(1)}, bf16[9,128,4,128]{3,1,2,0:T(8,128)(2,1)}, ...), branch_computations={%region_19.19_spmd, %region_20.20_spmd} | conditional | flops 676676352 | bytes 24192580 | solution.py:196
  332.1 7.3 %conditional.11 = (f32[128,4,8,128]{3,0,2,1:T(8,128)S(1)}, f32[1,2,128,512]{2,3,1,0:T(8,128)S(1)}) conditional(s32[]{:T(128)} %convert_element_type.108, f32[128,4,8,128]{3,0,2,1:T(8,128)S(1)} %get-tuple-element.1961, (s32[]{:T(128)}, s32[128]{0:T(128)S(1)}, s32[]{:T(128)}, s32[4]{0:T(128)S(1)}, bf16[9,128,4,128]{3,1,2,0:T(8,128)(2,1)}, ...), branch_computations={%region_19.19_spmd, %region_20.20_spmd} | conditional | flops 676676352 | bytes 24192580 | solution.py:196
  342.2 7.3 %conditional.11 = (f32[128,4,8,128]{3,0,2,1:T(8,128)S(1)}, f32[1,2,128,512]{2,3,1,0:T(8,128)S(1)}) conditional(s32[]{:T(128)} %convert_element_type.108, f32[128,4,8,128]{3,0,2,1:T(8,128)S(1)} %get-tuple-element.1961, (s32[]{:T(128)}, s32[128]{0:T(128)S(1)}, s32[]{:T(128)}, s32[4]{0:T(128)S(1)}, bf16[9,128,4,128]{3,1,2,0:T(8,128)(2,1)}, ...), branch_computations={%region_19.19_spmd, %region_20.20_spmd} | conditional | flops 676676352 | bytes 24192580 | solution.py:196
  352.2 7.3 %conditional.11 = (f32[128,4,8,128]{3,0,2,1:T(8,128)S(1)}, f32[1,2,128,512]{2,3,1,0:T(8,128)S(1)}) conditional(s32[]{:T(128)} %convert_element_type.108, f32[128,4,8,128]{3,0,2,1:T(8,128)S(1)} %get-tuple-element.1961, (s32[]{:T(128)}, s32[128]{0:T(128)S(1)}, s32[]{:T(128)}, s32[4]{0:T(128)S(1)}, bf16[9,128,4,128]{3,1,2,0:T(8,128)(2,1)}, ...), branch_computations={%region_19.19_spmd, %region_20.20_spmd} | conditional | flops 676676352 | bytes 24192580 | solution.py:196
  362.2 7.3 %conditional.11 = (f32[128,4,8,128]{3,0,2,1:T(8,128)S(1)}, f32[1,2,128,512]{2,3,1,0:T(8,128)S(1)}) conditional(s32[]{:T(128)} %convert_element_type.108, f32[128,4,8,128]{3,0,2,1:T(8,128)S(1)} %get-tuple-element.1961, (s32[]{:T(128)}, s32[128]{0:T(128)S(1)}, s32[]{:T(128)}, s32[4]{0:T(128)S(1)}, bf16[9,128,4,128]{3,1,2,0:T(8,128)(2,1)}, ...), branch_computations={%region_19.19_spmd, %region_20.20_spmd} | conditional | flops 676676352 | bytes 24192580 | solution.py:196
  372.2 7.3 %conditional.11 = (f32[128,4,8,128]{3,0,2,1:T(8,128)S(1)}, f32[1,2,128,512]{2,3,1,0:T(8,128)S(1)}) conditional(s32[]{:T(128)} %convert_element_type.108, f32[128,4,8,128]{3,0,2,1:T(8,128)S(1)} %get-tuple-element.1961, (s32[]{:T(128)}, s32[128]{0:T(128)S(1)}, s32[]{:T(128)}, s32[4]{0:T(128)S(1)}, bf16[9,128,4,128]{3,1,2,0:T(8,128)(2,1)}, ...), branch_computations={%region_19.19_spmd, %region_20.20_spmd} | conditional | flops 676676352 | bytes 24192580 | solution.py:196
  385.8 85.3 %while.90 = (s32[]{:T(128)}, f32[2,128,512]{2,1,0:T(8,128)S(1)}, f32[9,2,128,512]{2,3,1,0:T(8,128)}, s32[]{:T(128)}, s32[]{:T(128)}, /*index=5*/s32[]{:T(128)}) while((s32[]{:T(128)}, f32[2,128,512]{2,1,0:T(8,128)S(1)}, f32[9,2,128,512]{2,3,1,0:T(8,128)}, s32[]{:T(128)}, s32[]{:T(128)}, /*index=5*/s32[]{:T(128)}) %tuple.268), condition=%wide.region_23.24_spmd, body=%wide.region_22.23_spmd.sunk | while | flops 393221 | bytes 5243035 | solution.py:210
  385.9 3.7 collective-permute-start.1
  390.9 6.3 %collective-permute-done.1 = bf16[2,128,512]{2,1,0:T(8,128)(2,1)S(1)} collective-permute-done((bf16[2,128,512]{2,1,0:T(8,128)(2,1)S(1)}, bf16[2,128,512]{2,1,0:T(8,128)(2,1)S(1)}, u32[]{:S(2)}, u32[]{:S(2)}) %collective-permute-start.1) | collective-permute-done | bytes 262176 | tf_op jit(solution)/shard_map/while/body/eval_jaxpr/ppermute | solution.py:20
  400.5 7.2 %collective-permute-done.1 = bf16[2,128,512]{2,1,0:T(8,128)(2,1)S(1)} collective-permute-done((bf16[2,128,512]{2,1,0:T(8,128)(2,1)S(1)}, bf16[2,128,512]{2,1,0:T(8,128)(2,1)S(1)}, u32[]{:S(2)}, u32[]{:S(2)}) %collective-permute-start.1) | collective-permute-done | bytes 262176 | tf_op jit(solution)/shard_map/while/body/eval_jaxpr/ppermute | solution.py:20
  411.1 6.8 %collective-permute-done.1 = bf16[2,128,512]{2,1,0:T(8,128)(2,1)S(1)} collective-permute-done((bf16[2,128,512]{2,1,0:T(8,128)(2,1)S(1)}, bf16[2,128,512]{2,1,0:T(8,128)(2,1)S(1)}, u32[]{:S(2)}, u32[]{:S(2)}) %collective-permute-start.1) | collective-permute-done | bytes 262176 | tf_op jit(solution)/shard_map/while/body/eval_jaxpr/ppermute | solution.py:20
  421.3 6.8 %collective-permute-done.1 = bf16[2,128,512]{2,1,0:T(8,128)(2,1)S(1)} collective-permute-done((bf16[2,128,512]{2,1,0:T(8,128)(2,1)S(1)}, bf16[2,128,512]{2,1,0:T(8,128)(2,1)S(1)}, u32[]{:S(2)}, u32[]{:S(2)}) %collective-permute-start.1) | collective-permute-done | bytes 262176 | tf_op jit(solution)/shard_map/while/body/eval_jaxpr/ppermute | solution.py:20
  431.5 6.8 %collective-permute-done.1 = bf16[2,128,512]{2,1,0:T(8,128)(2,1)S(1)} collective-permute-done((bf16[2,128,512]{2,1,0:T(8,128)(2,1)S(1)}, bf16[2,128,512]{2,1,0:T(8,128)(2,1)S(1)}, u32[]{:S(2)}, u32[]{:S(2)}) %collective-permute-start.1) | collective-permute-done | bytes 262176 | tf_op jit(solution)/shard_map/while/body/eval_jaxpr/ppermute | solution.py:20
  441.7 7.3 %collective-permute-done.1 = bf16[2,128,512]{2,1,0:T(8,128)(2,1)S(1)} collective-permute-done((bf16[2,128,512]{2,1,0:T(8,128)(2,1)S(1)}, bf16[2,128,512]{2,1,0:T(8,128)(2,1)S(1)}, u32[]{:S(2)}, u32[]{:S(2)}) %collective-permute-start.1) | collective-permute-done | bytes 262176 | tf_op jit(solution)/shard_map/while/body/eval_jaxpr/ppermute | solution.py:20
  452.4 8.5 %collective-permute-done.1 = bf16[2,128,512]{2,1,0:T(8,128)(2,1)S(1)} collective-permute-done((bf16[2,128,512]{2,1,0:T(8,128)(2,1)S(1)}, bf16[2,128,512]{2,1,0:T(8,128)(2,1)S(1)}, u32[]{:S(2)}, u32[]{:S(2)}) %collective-permute-start.1) | collective-permute-done | bytes 262176 | tf_op jit(solution)/shard_map/while/body/eval_jaxpr/ppermute | solution.py:20
  464.2 6.8 %collective-permute-done.1 = bf16[2,128,512]{2,1,0:T(8,128)(2,1)S(1)} collective-permute-done((bf16[2,128,512]{2,1,0:T(8,128)(2,1)S(1)}, bf16[2,128,512]{2,1,0:T(8,128)(2,1)S(1)}, u32[]{:S(2)}, u32[]{:S(2)}) %collective-permute-start.1) | collective-permute-done | bytes 262176 | tf_op jit(solution)/shard_map/while/body/eval_jaxpr/ppermute | solution.py:20
  (494 shorter events, 279.9 us)
Async XLA Ops:
  7.2 186.1 %all-gather.3.cloned.1.call-start = ((), (), s32[]{:S(2)}) async-start(), calls=%async_computation | async-start | bytes 2228224 | tf_op jit(solution)/shard_map/all_gather | solution.py:77
  8.9 184.4 %all-gather.5.cloned.1.call-start = ((), (), s32[]{:S(2)}) async-start(), calls=%async_computation.1 | async-start | bytes 2228224 | tf_op jit(solution)/shard_map/all_gather | solution.py:78
  10.6 2.4 copy-start.5
  10.7 2.4 copy-start.6
  12.3 115.1 %copy-start = (bf16[128,4096]{0,1:T(8,128)(2,1)}, bf16[128,4096]{0,1:T(8,128)(2,1)S(1)}, u32[]{:S(2)}) copy-start(bf16[128,4096]{0,1:T(8,128)(2,1)S(1)} %copy.32) | copy-start | bytes 3145732
  15.0 11.5 %collective-permute-start = (bf16[2,128,512]{2,1,0:T(8,128)(2,1)}, bf16[2,128,512]{2,1,0:T(8,128)(2,1)S(1)}, u32[]{:S(2)}, u32[]{:S(2)}) collective-permute-start(bf16[2,128,512]{2,1,0:T(8,128)(2,1)} %get-tuple-element.1881), channel_id=1, source_target_pairs={{0,2},{2,4},{4,6},{6,8},{8,10},{10,12},{12,14},{14,16},{16,18},{18... | collective-permute-start | bytes 786440 | tf_op jit(solution)/shard_map/while/body/eval_jaxpr/ppermute | solution.py:20
  27.9 9.6 %collective-permute-start = (bf16[2,128,512]{2,1,0:T(8,128)(2,1)}, bf16[2,128,512]{2,1,0:T(8,128)(2,1)S(1)}, u32[]{:S(2)}, u32[]{:S(2)}) collective-permute-start(bf16[2,128,512]{2,1,0:T(8,128)(2,1)} %get-tuple-element.1881), channel_id=1, source_target_pairs={{0,2},{2,4},{4,6},{6,8},{8,10},{10,12},{12,14},{14,16},{16,18},{18... | collective-permute-start | bytes 786440 | tf_op jit(solution)/shard_map/while/body/eval_jaxpr/ppermute | solution.py:20
  38.9 12.9 %collective-permute-start = (bf16[2,128,512]{2,1,0:T(8,128)(2,1)}, bf16[2,128,512]{2,1,0:T(8,128)(2,1)S(1)}, u32[]{:S(2)}, u32[]{:S(2)}) collective-permute-start(bf16[2,128,512]{2,1,0:T(8,128)(2,1)} %get-tuple-element.1881), channel_id=1, source_target_pairs={{0,2},{2,4},{4,6},{6,8},{8,10},{10,12},{12,14},{14,16},{16,18},{18... | collective-permute-start | bytes 786440 | tf_op jit(solution)/shard_map/while/body/eval_jaxpr/ppermute | solution.py:20
  53.2 19.2 %collective-permute-start = (bf16[2,128,512]{2,1,0:T(8,128)(2,1)}, bf16[2,128,512]{2,1,0:T(8,128)(2,1)S(1)}, u32[]{:S(2)}, u32[]{:S(2)}) collective-permute-start(bf16[2,128,512]{2,1,0:T(8,128)(2,1)} %get-tuple-element.1881), channel_id=1, source_target_pairs={{0,2},{2,4},{4,6},{6,8},{8,10},{10,12},{12,14},{14,16},{16,18},{18... | collective-permute-start | bytes 786440 | tf_op jit(solution)/shard_map/while/body/eval_jaxpr/ppermute | solution.py:20
  73.8 12.3 %collective-permute-start = (bf16[2,128,512]{2,1,0:T(8,128)(2,1)}, bf16[2,128,512]{2,1,0:T(8,128)(2,1)S(1)}, u32[]{:S(2)}, u32[]{:S(2)}) collective-permute-start(bf16[2,128,512]{2,1,0:T(8,128)(2,1)} %get-tuple-element.1881), channel_id=1, source_target_pairs={{0,2},{2,4},{4,6},{6,8},{8,10},{10,12},{12,14},{14,16},{16,18},{18... | collective-permute-start | bytes 786440 | tf_op jit(solution)/shard_map/while/body/eval_jaxpr/ppermute | solution.py:20
  87.4 10.3 %collective-permute-start = (bf16[2,128,512]{2,1,0:T(8,128)(2,1)}, bf16[2,128,512]{2,1,0:T(8,128)(2,1)S(1)}, u32[]{:S(2)}, u32[]{:S(2)}) collective-permute-start(bf16[2,128,512]{2,1,0:T(8,128)(2,1)} %get-tuple-element.1881), channel_id=1, source_target_pairs={{0,2},{2,4},{4,6},{6,8},{8,10},{10,12},{12,14},{14,16},{16,18},{18... | collective-permute-start | bytes 786440 | tf_op jit(solution)/shard_map/while/body/eval_jaxpr/ppermute | solution.py:20
  99.0 10.4 %collective-permute-start = (bf16[2,128,512]{2,1,0:T(8,128)(2,1)}, bf16[2,128,512]{2,1,0:T(8,128)(2,1)S(1)}, u32[]{:S(2)}, u32[]{:S(2)}) collective-permute-start(bf16[2,128,512]{2,1,0:T(8,128)(2,1)} %get-tuple-element.1881), channel_id=1, source_target_pairs={{0,2},{2,4},{4,6},{6,8},{8,10},{10,12},{12,14},{14,16},{16,18},{18... | collective-permute-start | bytes 786440 | tf_op jit(solution)/shard_map/while/body/eval_jaxpr/ppermute | solution.py:20
  110.8 13.0 %collective-permute-start = (bf16[2,128,512]{2,1,0:T(8,128)(2,1)}, bf16[2,128,512]{2,1,0:T(8,128)(2,1)S(1)}, u32[]{:S(2)}, u32[]{:S(2)}) collective-permute-start(bf16[2,128,512]{2,1,0:T(8,128)(2,1)} %get-tuple-element.1881), channel_id=1, source_target_pairs={{0,2},{2,4},{4,6},{6,8},{8,10},{10,12},{12,14},{14,16},{16,18},{18... | collective-permute-start | bytes 786440 | tf_op jit(solution)/shard_map/while/body/eval_jaxpr/ppermute | solution.py:20
  125.2 1.0 copy-start.3
  127.5 3.8 copy-start.7
  128.7 2.7 copy-start.4
  131.4 1.7 copy-start.8
  240.5 2.2 copy-start.2
  297.6 1.2 copy-start.1
  307.6 1.2 copy-start.1
  317.6 1.2 copy-start.1
  327.7 1.2 copy-start.1
  337.7 1.2 copy-start.1
  347.7 1.2 copy-start.1
  357.8 1.2 copy-start.1
  367.8 1.2 copy-start.1
  377.8 1.2 copy-start.1
  385.9 11.3 %collective-permute-start.1 = (bf16[2,128,512]{2,1,0:T(8,128)(2,1)S(1)}, bf16[2,128,512]{2,1,0:T(8,128)(2,1)S(1)}, u32[]{:S(2)}, u32[]{:S(2)}) collective-permute-start(bf16[2,128,512]{2,1,0:T(8,128)(2,1)S(1)} %convert_element_type.105), channel_id=1, source_target_pairs={{2,0},{4,2},{6,4},{8,6},{10,8},{12,10},{14,12},{16,14},{18,16},{20... | collective-permute-start | bytes 786440 | tf_op jit(solution)/shard_map/while/body/eval_jaxpr/ppermute | solution.py:20
  397.3 10.4 %collective-permute-start.1 = (bf16[2,128,512]{2,1,0:T(8,128)(2,1)S(1)}, bf16[2,128,512]{2,1,0:T(8,128)(2,1)S(1)}, u32[]{:S(2)}, u32[]{:S(2)}) collective-permute-start(bf16[2,128,512]{2,1,0:T(8,128)(2,1)S(1)} %convert_element_type.105), channel_id=1, source_target_pairs={{2,0},{4,2},{6,4},{8,6},{10,8},{12,10},{14,12},{16,14},{18,16},{20... | collective-permute-start | bytes 786440 | tf_op jit(solution)/shard_map/while/body/eval_jaxpr/ppermute | solution.py:20
  407.9 10.1 %collective-permute-start.1 = (bf16[2,128,512]{2,1,0:T(8,128)(2,1)S(1)}, bf16[2,128,512]{2,1,0:T(8,128)(2,1)S(1)}, u32[]{:S(2)}, u32[]{:S(2)}) collective-permute-start(bf16[2,128,512]{2,1,0:T(8,128)(2,1)S(1)} %convert_element_type.105), channel_id=1, source_target_pairs={{2,0},{4,2},{6,4},{8,6},{10,8},{12,10},{14,12},{16,14},{18,16},{20... | collective-permute-start | bytes 786440 | tf_op jit(solution)/shard_map/while/body/eval_jaxpr/ppermute | solution.py:20
  418.1 10.1 %collective-permute-start.1 = (bf16[2,128,512]{2,1,0:T(8,128)(2,1)S(1)}, bf16[2,128,512]{2,1,0:T(8,128)(2,1)S(1)}, u32[]{:S(2)}, u32[]{:S(2)}) collective-permute-start(bf16[2,128,512]{2,1,0:T(8,128)(2,1)S(1)} %convert_element_type.105), channel_id=1, source_target_pairs={{2,0},{4,2},{6,4},{8,6},{10,8},{12,10},{14,12},{16,14},{18,16},{20... | collective-permute-start | bytes 786440 | tf_op jit(solution)/shard_map/while/body/eval_jaxpr/ppermute | solution.py:20
  428.3 10.1 %collective-permute-start.1 = (bf16[2,128,512]{2,1,0:T(8,128)(2,1)S(1)}, bf16[2,128,512]{2,1,0:T(8,128)(2,1)S(1)}, u32[]{:S(2)}, u32[]{:S(2)}) collective-permute-start(bf16[2,128,512]{2,1,0:T(8,128)(2,1)S(1)} %convert_element_type.105), channel_id=1, source_target_pairs={{2,0},{4,2},{6,4},{8,6},{10,8},{12,10},{14,12},{16,14},{18,16},{20... | collective-permute-start | bytes 786440 | tf_op jit(solution)/shard_map/while/body/eval_jaxpr/ppermute | solution.py:20
  438.5 10.6 %collective-permute-start.1 = (bf16[2,128,512]{2,1,0:T(8,128)(2,1)S(1)}, bf16[2,128,512]{2,1,0:T(8,128)(2,1)S(1)}, u32[]{:S(2)}, u32[]{:S(2)}) collective-permute-start(bf16[2,128,512]{2,1,0:T(8,128)(2,1)S(1)} %convert_element_type.105), channel_id=1, source_target_pairs={{2,0},{4,2},{6,4},{8,6},{10,8},{12,10},{14,12},{16,14},{18,16},{20... | collective-permute-start | bytes 786440 | tf_op jit(solution)/shard_map/while/body/eval_jaxpr/ppermute | solution.py:20
  449.2 11.7 %collective-permute-start.1 = (bf16[2,128,512]{2,1,0:T(8,128)(2,1)S(1)}, bf16[2,128,512]{2,1,0:T(8,128)(2,1)S(1)}, u32[]{:S(2)}, u32[]{:S(2)}) collective-permute-start(bf16[2,128,512]{2,1,0:T(8,128)(2,1)S(1)} %convert_element_type.105), channel_id=1, source_target_pairs={{2,0},{4,2},{6,4},{8,6},{10,8},{12,10},{14,12},{16,14},{18,16},{20... | collective-permute-start | bytes 786440 | tf_op jit(solution)/shard_map/while/body/eval_jaxpr/ppermute | solution.py:20
  461.0 10.1 %collective-permute-start.1 = (bf16[2,128,512]{2,1,0:T(8,128)(2,1)S(1)}, bf16[2,128,512]{2,1,0:T(8,128)(2,1)S(1)}, u32[]{:S(2)}, u32[]{:S(2)}) collective-permute-start(bf16[2,128,512]{2,1,0:T(8,128)(2,1)S(1)} %convert_element_type.105), channel_id=1, source_target_pairs={{2,0},{4,2},{6,4},{8,6},{10,8},{12,10},{14,12},{16,14},{18,16},{20... | collective-permute-start | bytes 786440 | tf_op jit(solution)/shard_map/while/body/eval_jaxpr/ppermute | solution.py:20
Sparse Core Ops, SparseCore 0:
  11.2 72.0 all-gather.2
  86.0 67.3 all-gather.4
where the time goes:
time: 484 us; the launch traced here: 481 us
  matrix products  111 us (23%)
  waiting for transfers between devices  110 us (23%)
  local copies, waits for them, and re-layouts  82.4 us (17%)
  starting transfers between devices  63.5 us (13%)
  blocking collectives  45.9 us (9%)
  loops' own time  26.5 us (5%)
  other arithmetic  25.4 us (5%)
  between operations  16.7 us (3%)
    ppermute x16, waiting for transfers between devices, passed_along(): lax.ppermute(value, axis, [(source, source + steps) for source in range(f...  110 us
    ppermute x16, starting transfers between devices, passed_along(): lax.ppermute(value, axis, [(source, source + steps) for source in range(f...  63.4 us
    psum x1, blocking collectives, body(): square_total = lax.psum(jnp.sum(difference * difference), ('ctx', 'head'))  45.9 us
    dot_general x21, matrix products, tile_update(): jnp.einsum('tngs,snd->tngd', weights.astype(jnp.bfloat16), block_values,...  37.3 us
    dot_general x21, matrix products, tile_update(): jnp.einsum('tngd,snd->tngs', query_block, block_keys, preferred_element_t...  18.5 us
    dot_general x9, matrix products, active(): jnp.einsum('tngd,snd->tngs', local_q, block_keys, preferred_element_type=...  17.5 us
    dot_general x9, matrix products, active(): jnp.einsum('tngs,snd->tngd', grad_s, block_keys, preferred_element_type=j...  17.3 us
    unnamed x23, local copies, waits for them, and re-layouts  13.9 us
  transfers between devices with their start and end apart: 18, of which 16 were waited for; matrix products, arithmetic and copies ran while one was open for 17% of the time, Pallas kernels for 0%

commit v1 on v0

v1 whole, which is shorter than its diff:
```python
import functools
import math

import jax
import jax.numpy as jnp
from jax import lax
from jax.experimental import pallas as pl
from jax.experimental.pallas import tpu as pltpu
from jax.sharding import PartitionSpec as P

QH = 64
KVH = 8
HD = 128
WIN_MAX = 1024
WIN_MIN = 512
GS = QH // KVH

MESH = pl.DeviceIdType.MESH
NEG = -1e30
FLOOR = -1e20
F32 = jnp.float32
BF16 = jnp.bfloat16


def dot_nt(a, b):
    return lax.dot_general(a, b, (((1,), (1,)), ((), ())), preferred_element_type=F32)


def dot_nn(a, b):
    return jnp.dot(a, b, preferred_element_type=F32)


def kernel(
    G, NB, SH, T, D,
    w_ref, q_ref, k_ref, v_ref,
    dq_out, dkv_out, loss_out,
    qs, kvs, kts, vts, o_near, o_far, stats, dos, dqs, dkv_acc, dkv_send, dkv_recv, dkv_fin, loss_acc,
    q_send, q_recv, k_send, k_recv, v_send, v_recv, kv_send, kv_recv,
    g_send, g_recv, dq_send, dq_recv, f_send, f_recv, loc,
):
    R = G * SH
    NT = R // T
    QW = GS * HD
    me = lax.axis_index("ctx")
    z = me // G
    p = lax.rem(me, G)
    c = math.log2(math.e) / math.sqrt(HD)
    inv_root = 1.0 / math.sqrt(HD)

    def dev(zz, pp):
        return {"ctx": zz * G + pp}

    barrier = pltpu.get_barrier_semaphore()
    for o in range(1, G):
        pl.semaphore_signal(barrier, inc=1, device_id=dev(z, lax.rem(p + o, G)), device_id_type=MESH)

    def greet(o, carry):
        pl.semaphore_signal(barrier, inc=1, device_id=dev(lax.rem(z + o, NB), p), device_id_type=MESH)
        return carry

    lax.fori_loop(1, NB, greet, 0)
    pl.semaphore_wait(barrier, G - 1 + NB - 1)

    def my_rows(pp):
        return pl.ds(pl.multiple_of(pp * SH, SH), SH)

    def wide(pp):
        return pl.ds(pl.multiple_of(pp * QW, QW), QW)

    def narrow(pp):
        return pl.ds(pl.multiple_of(pp * HD, HD), HD)

    def kv_copy(src, part, o, send, recv):
        to = lax.rem(p + o, G)
        return pltpu.make_async_remote_copy(
            src_ref=src.at[:, narrow(to)],
            dst_ref=kvs.at[z, part, my_rows(p), :],
            send_sem=send.at[to], recv_sem=recv.at[p],
            device_id=dev(z, to), device_id_type=MESH)

    def q_copy(o):
        to = lax.rem(p + o, G)
        return pltpu.make_async_remote_copy(
            src_ref=q_ref.at[:, wide(to)],
            dst_ref=qs.at[my_rows(p), :],
            send_sem=q_send.at[to], recv_sem=q_recv.at[p],
            device_id=dev(z, to), device_id_type=MESH)

    def recv_kv(frm, part, recv):
        return pltpu.make_async_remote_copy(
            src_ref=kvs.at[z, part, my_rows(frm), :], dst_ref=kvs.at[z, part, my_rows(frm), :],
            send_sem=k_send.at[frm], recv_sem=recv.at[frm],
            device_id=dev(z, frm), device_id_type=MESH)

    for o in range(1, G):
        kv_copy(k_ref, 0, o, k_send, k_recv).start()
        kv_copy(v_ref, 1, o, v_send, v_recv).start()
    for o in range(1, G):
        q_copy(o).start()
    local = [
        pltpu.make_async_copy(k_ref.at[:, narrow(p)], kvs.at[z, 0, my_rows(p), :], loc.at[0]),
        pltpu.make_async_copy(v_ref.at[:, narrow(p)], kvs.at[z, 1, my_rows(p), :], loc.at[1]),
        pltpu.make_async_copy(q_ref.at[:, wide(p)], qs.at[my_rows(p), :], loc.at[2]),
    ]
    for one in local:
        one.start()

    stats[...] = jnp.zeros_like(stats)
    loss_acc[...] = jnp.zeros_like(loss_acc)

    def clear(h, carry):
        o_far[h] = jnp.zeros(o_far.shape[1:], F32)
        stats[h, pl.ds(2, 1), :] = jnp.full((1, R), FLOOR, F32)
        return carry

    lax.fori_loop(0, GS, clear, 0)

    for one in local:
        one.wait()
    for o in range(1, G):
        frm = lax.rem(p + o, G)
        recv_kv(frm, 0, k_recv).wait_recv()
        recv_kv(frm, 1, v_recv).wait_recv()

    def block_copy(src_block, to_z):
        return pltpu.make_async_remote_copy(
            src_ref=kvs.at[src_block], dst_ref=kvs.at[src_block],
            send_sem=kv_send.at[to_z], recv_sem=kv_recv.at[src_block],
            device_id=dev(to_z, p), device_id_type=MESH)

    def send_up(to_z, carry):
        block_copy(z, to_z).start()
        return carry

    lax.fori_loop(z + 1, NB, send_up, 0)
    for o in range(1, G):
        frm = lax.rem(p + o, G)
        pltpu.make_async_remote_copy(
            src_ref=qs.at[my_rows(frm), :], dst_ref=qs.at[my_rows(frm), :],
            send_sem=q_send.at[frm], recv_sem=q_recv.at[frm],
            device_id=dev(z, frm), device_id_type=MESH).wait_recv()

    window = w_ref[p]
    ramp = lax.broadcasted_iota(jnp.int32, (T, T), 1) - lax.broadcasted_iota(jnp.int32, (T, T), 0)

    def tiles_of(d, rt):
        found = []
        for kt in range(NT):
            delta = d * R + (rt - kt) * T
            if delta < 0:
                continue
            near = delta - (T - 1) < WIN_MAX
            far = delta + (T - 1) >= WIN_MIN
            found.append((kt, delta, near, far))
        return found

    def turn(ref_out, block, part):
        ref_out[...] = kvs[block, part].astype(F32).T.astype(BF16)

    def forward(h, d, rt, block, far_only=False):
        rows = slice(rt * T, (rt + 1) * T)
        q = qs[rows, narrow(h)]
        work = []
        for kt, delta, near, far in ([(kt, None, False, True) for kt in range(NT)] if far_only else tiles_of(d, rt)):
            keys = kvs[block, 0, kt * T:(kt + 1) * T, :]
            work.append((kt, delta, near, far, dot_nt(keys, q) * c))
        has_near = any(t[2] for t in work)
        has_far = any(t[3] for t in work)
        if has_near:
            m_s = None if d == 0 else stats[h, 0:1, rows]
            new_s = m_s
        if has_far:
            m_f = stats[h, 2:3, rows]
            new_f = m_f
        masks = []
        for kt, delta, near, far, s in work:
            mask = None
            if near and far:
                mask = ramp < window - delta
                s_near = jnp.where(mask, s, NEG)
                s_far = jnp.where(mask, NEG, s)
            elif near and delta == 0:
                s_near = jnp.where(ramp >= 0, s, NEG)
                mask = s_near
            else:
                s_near = s_far = s
            masks.append(mask)
            if near:
                top = jnp.max(s_near, axis=0, keepdims=True)
                new_s = top if new_s is None else jnp.maximum(new_s, top)
            if far:
                new_f = jnp.maximum(new_f, jnp.max(s_far, axis=0, keepdims=True))
        near_sum, far_sum, near_o, far_o = 0.0, 0.0, 0.0, 0.0
        for (kt, delta, near, far, s), mask in zip(work, masks):
            vt = vts[:, kt * T:(kt + 1) * T]
            if near and far:
                e = jnp.exp2(s - jnp.where(mask, new_s, new_f))
                p_near = jnp.where(mask, e, 0.0)
                p_far = jnp.where(mask, 0.0, e)
            elif near:
                p_near = jnp.exp2((mask if delta == 0 else s) - new_s)
            else:
                p_far = jnp.exp2(s - new_f)
            if near:
                near_sum = near_sum + jnp.sum(p_near, axis=0, keepdims=True)
                near_o = near_o + dot_nn(vt, p_near.astype(BF16))
            if far:
                far_sum = far_sum + jnp.sum(p_far, axis=0, keepdims=True)
                far_o = far_o + dot_nn(vt, p_far.astype(BF16))
        if has_near:
            if d == 0:
                stats[h, 1:2, rows] = near_sum
                o_near[h, :, rows] = near_o
            else:
                factor = jnp.exp2(m_s - new_s)
                stats[h, 1:2, rows] = stats[h, 1:2, rows] * factor + near_sum
                o_near[h, :, rows] = o_near[h, :, rows] * factor + near_o
            stats[h, 0:1, rows] = new_s
        if has_far:
            factor = jnp.exp2(m_f - new_f)
            stats[h, 3:4, rows] = stats[h, 3:4, rows] * factor + far_sum
            o_far[h, :, rows] = o_far[h, :, rows] * factor + far_o
            stats[h, 2:3, rows] = new_f

    def heads(fn):
        def step(h, carry):
            fn(h)
            return carry
        lax.fori_loop(0, GS, step, 0)

    def arrive(block):
        block_copy(block, z).wait_recv()

    for d in range(0, min(D, NB - 1) + 1):
        @pl.when(z >= d)
        def _():
            block = z - d
            if d > 0:
                arrive(block)
            turn(vts, block, 1)
            for rt in range(NT):
                heads(lambda h: forward(h, d, rt, block))

    if NB - 1 > D:
        def far_block(d, carry):
            block = z - d
            arrive(block)
            turn(vts, block, 1)
            for rt in range(NT):
                heads(lambda h: forward(h, None, rt, block, True))
            return carry
        lax.fori_loop(D + 1, z + 1, far_block, 0)

    def middle(h, rt):
        rows = slice(rt * T, (rt + 1) * T)
        m_s, l_s = stats[h, 0:1, rows], stats[h, 1:2, rows]
        m_f, l_f = stats[h, 2:3, rows], stats[h, 3:4, rows]
        m_t = jnp.maximum(m_s, m_f)
        a_s, a_f = jnp.exp2(m_s - m_t), jnp.exp2(m_f - m_t)
        total = l_s * a_s + l_f * a_f
        near = o_near[h, :, rows]
        student = near / l_s
        teacher = (near * a_s + o_far[h, :, rows] * a_f) / total
        diff = student - teacher.astype(BF16).astype(F32)
        loss_acc[...] += jnp.sum((diff * diff).reshape(HD // 8, 8, T), axis=0)
        stats[h, 4:5, rows] = m_s + jnp.log2(l_s)
        stats[h, 5:6, rows] = jnp.sum(diff * student, axis=0, keepdims=True)
        dos[rows, narrow(h)] = diff.T.astype(BF16)
        o_near[h, :, rows] = jnp.zeros((HD, T), F32)

    for rt in range(NT):
        heads(lambda h: middle(h, rt))
    loss_out[...] = loss_acc[...]

    def backward(h, d, rt, block):
        rows = slice(rt * T, (rt + 1) * T)
        q = qs[rows, narrow(h)]
        do = dos[rows, narrow(h)]
        lse = stats[h, 4:5, rows]
        rd = stats[h, 5:6, rows]
        dq = o_near[h, :, rows]
        for kt, delta, near, far in tiles_of(d, rt):
            if not near:
                continue
            part = slice(kt * T, (kt + 1) * T)
            s = dot_nt(kvs[block, 0, part, :], q) * c
            if far:
                s = jnp.where(ramp < window - delta, s, NEG)
            elif delta == 0:
                s = jnp.where(ramp >= 0, s, NEG)
            w = jnp.exp2(s - lse)
            dp = dot_nt(kvs[block, 1, part, :], do)
            ds = (w * (dp - rd)).astype(BF16)
            dkv_acc[1, part, :] += dot_nn(w.astype(BF16), do)
            dkv_acc[0, part, :] += dot_nn(ds, q)
            dq = dq + dot_nn(kts[:, part], ds)
        if d == 0:
            dqs[rows, narrow(h)] = (dq * inv_root).T.astype(BF16)
        else:
            o_near[h, :, rows] = dq

    def term_copy(d, to_z):
        return pltpu.make_async_remote_copy(
            src_ref=dkv_send.at[d - 1], dst_ref=dkv_recv.at[d - 1],
            send_sem=g_send.at[d - 1], recv_sem=g_recv.at[d - 1],
            device_id=dev(to_z, p), device_id_type=MESH)

    def dq_copy(to):
        return pltpu.make_async_remote_copy(
            src_ref=dqs.at[my_rows(to), :], dst_ref=dq_out.at[p],
            send_sem=dq_send.at[to], recv_sem=dq_recv.at[p],
            device_id=dev(z, to), device_id_type=MESH)

    def dq_local(to):
        return pltpu.make_async_copy(dqs.at[my_rows(to), :], dq_out.at[p], loc.at[2])

    def fin_copy(to):
        return pltpu.make_async_remote_copy(
            src_ref=dkv_fin.at[:, my_rows(to), :], dst_ref=dkv_out.at[p],
            send_sem=f_send.at[to], recv_sem=f_recv.at[p],
            device_id=dev(z, to), device_id_type=MESH)

    def fin_local(to):
        return pltpu.make_async_copy(dkv_fin.at[:, my_rows(to), :], dkv_out.at[p], loc.at[3])

    for d in range(min(D, NB - 1), 0, -1):
        @pl.when(z >= d)
        def _():
            block = z - d
            dkv_acc[...] = jnp.zeros_like(dkv_acc)
            turn(kts, block, 0)
            for rt in range(NT):
                if any(t[2] for t in tiles_of(d, rt)):
                    heads(lambda h: backward(h, d, rt, block))
            dkv_send[d - 1, 0] = (dkv_acc[0] * inv_root).astype(BF16)
            dkv_send[d - 1, 1] = dkv_acc[1].astype(BF16)
            term_copy(d, z - d).start()

    dkv_acc[...] = jnp.zeros_like(dkv_acc)
    turn(kts, z, 0)
    for rt in range(NT):
        heads(lambda h: backward(h, 0, rt, z))
        for to in range(rt * T // SH, (rt + 1) * T // SH):
            @pl.when(p != to)
            def _():
                dq_copy(to).start()

            @pl.when(p == to)
            def _():
                dq_local(to).start()

    dkv_acc[0] = dkv_acc[0] * inv_root
    for d in range(1, min(D, NB - 1) + 1):
        @pl.when(z + d < NB)
        def _():
            term_copy(d, z).wait_recv()
            dkv_acc[...] += dkv_recv[d - 1].astype(F32)
    dkv_fin[...] = dkv_acc[...].astype(BF16)
    for to in range(G):
        @pl.when(p != to)
        def _():
            fin_copy(to).start()

        @pl.when(p == to)
        def _():
            fin_local(to).start()

    def drain_up(to_z, carry):
        block_copy(z, to_z).wait_send()
        return carry

    for o in range(1, G):
        kv_copy(k_ref, 0, o, k_send, k_recv).wait_send()
        kv_copy(v_ref, 1, o, v_send, v_recv).wait_send()
        q_copy(o).wait_send()
    lax.fori_loop(z + 1, NB, drain_up, 0)
    for d in range(1, min(D, NB - 1) + 1):
        @pl.when(z >= d)
        def _():
            term_copy(d, z - d).wait_send()
    dq_local(p).wait()
    fin_local(p).wait()
    for o in range(1, G):
        other = lax.rem(p + o, G)
        dq_copy(other).wait_send()
        fin_copy(other).wait_send()
        pltpu.make_async_remote_copy(
            src_ref=dq_out.at[other], dst_ref=dq_out.at[other],
            send_sem=dq_send.at[other], recv_sem=dq_recv.at[other],
            device_id=dev(z, other), device_id_type=MESH).wait_recv()
        pltpu.make_async_remote_copy(
            src_ref=dkv_out.at[other], dst_ref=dkv_out.at[other],
            send_sem=f_send.at[other], recv_sem=f_recv.at[other],
            device_id=dev(z, other), device_id_type=MESH).wait_recv()


def body(queries, keys, values, window):
    sh, key_width = keys.shape
    G = key_width // HD
    n_ctx = lax.axis_size("ctx")
    NB = n_ctx // G
    R = G * sh
    T = math.gcd(R, 256)
    D = (WIN_MAX - 1 + R - 1) // R
    DS = max(1, min(D, NB - 1))
    dma = pltpu.SemaphoreType.DMA
    any_spec = pl.BlockSpec(memory_space=pl.ANY)
    dq, dkv, loss_part = pl.pallas_call(
        functools.partial(kernel, G, NB, sh, T, D),
        out_shape=(
            jax.ShapeDtypeStruct((G, sh, GS * HD), BF16),
            jax.ShapeDtypeStruct((G, 2, sh, HD), BF16),
            jax.ShapeDtypeStruct((8, T), F32),
        ),
        in_specs=[pl.BlockSpec(memory_space=pltpu.SMEM), any_spec, any_spec, any_spec],
        out_specs=(any_spec, any_spec, pl.BlockSpec(memory_space=pltpu.VMEM)),
        scratch_shapes=[
            pltpu.VMEM((R, GS * HD), BF16),
            pltpu.VMEM((NB, 2, R, HD), BF16),
            pltpu.VMEM((HD, R), BF16),
            pltpu.VMEM((HD, R), BF16),
            pltpu.VMEM((GS, HD, R), F32),
            pltpu.VMEM((GS, HD, R), F32),
            pltpu.VMEM((GS, 8, R), F32),
            pltpu.VMEM((R, GS * HD), BF16),
            pltpu.VMEM((R, GS * HD), BF16),
            pltpu.VMEM((2, R, HD), F32),
            pltpu.VMEM((DS, 2, R, HD), BF16),
            pltpu.VMEM((DS, 2, R, HD), BF16),
            pltpu.VMEM((2, R, HD), BF16),
            pltpu.VMEM((8, T), F32),
            dma((G,)), dma((G,)), dma((G,)), dma((G,)), dma((G,)), dma((G,)),
            dma((NB,)), dma((NB,)),
            dma((DS,)), dma((DS,)),
            dma((G,)), dma((G,)), dma((G,)), dma((G,)),
            dma((4,)),
        ],
        compiler_params=pltpu.CompilerParams(
            collective_id=0, has_side_effects=True, vmem_limit_bytes=56 * 1024 * 1024),
    )(window, queries, keys, values)
    loss = lax.psum(jnp.sum(loss_part), ("ctx", "head")) / (sh * n_ctx * QH * HD)
    grad_q = dq.transpose(1, 0, 2).reshape(sh, -1).astype(F32)
    grads = dkv.transpose(1, 2, 0, 3).reshape(2, sh, -1).astype(F32)
    return (loss, grad_q, grads[0], grads[1])


def solution(mesh):
    return jax.shard_map(
        body,
        mesh=mesh,
        in_specs=(P("ctx", "head"), P("ctx", "head"), P("ctx", "head"), P("head")),
        out_specs=(P(), P("ctx", "head"), P("ctx", "head"), P("ctx", "head")),
        check_vma=False,
    )
```

time: 484 us -> 158 us (0.33)
  the two profiles are of different devices: /device:TPU:22 before, /device:TPU:28 now
where the time goes in v1:
time: 158 us; the launch traced here: 155 us
  Pallas kernels  105 us (66%)
  blocking collectives  38.3 us (24%)
  local copies, waits for them, and re-layouts  6.76 us (4%)
  other arithmetic  2.8 us (2%)
  between operations  2.46 us (2%)
    pallas_call x1, Pallas kernels, body(): pl.pallas_call(functools.partial(kernel, G, NB, sh, T, D), out_shape=(jax...  105 us
    psum x1, blocking collectives, body(): lax.psum(jnp.sum(loss_part), ('ctx', 'head')) / (sh * n_ctx * QH * HD)  38.3 us
    unnamed x5, local copies, waits for them, and re-layouts  4.6 us

profile of v1, /device:TPU:28, one launch (start us, length us, event | category | flops | bytes accessed | tf_op | source)
XLA Modules:
  0.0 155.1 jit_solution(17148988086027736269)
XLA Ops:
  0.6 104.8 %shard_map.75 = (bf16[4,128,1024]{2,1,0:T(8,128)(2,1)}, bf16[4,2,128,128]{3,2,1,0:T(8,128)(2,1)}, f32[8,256]{1,0:T(8,128)}) custom-call(s32[4]{0:T(128)} %w_ref.1, bf16[128,4096]{1,0:T(8,128)(2,1)} %q_ref.1, bf16[128,512]{1,0:T(8,128)(2,1)} %k_ref.1, bf16[128,512]{1,0:T(8,128)(2,1)} %v_ref.1), custom_call_target="tpu_custom_call" | custom-call | tf_op jit(solution)/shard_map/pallas_call | solution.py:408
  105.5 1.3 reduce_sum.9
  106.8 38.3 %psum.7 = f32[]{:T(128)} all-reduce(f32[]{:T(128)} %reduce_sum.9), channel_id=1, replica_groups=mesh['ctx'=16,'head'=2] {'ctx','head'}, use_global_device_ids=true, to_apply=%region_1.0 | all-reduce | flops 1 | bytes 8 | tf_op jit(solution)/shard_map/psum | solution.py:441
  145.7 1.5 convert_bitcast_fusion
  147.2 1.9 %copy.8 = f32[128,4,1024]{0,2,1:T(8,128)} copy(f32[128,4,1024]{2,0,1:T(8,128)S(1)} %convert_bitcast_fusion) | data formatting | bytes 4194304 | tf_op jit(solution)/shard_map/convert_element_type | solution.py:442
  149.0 0.0 copy-start
  149.0 2.9 %copy.11 = f32[128,4096]{1,0:T(8,128)} copy(f32[128,4096]{0,1:T(8,128)} %bitcast.7) | data formatting | bytes 4194304
  152.0 0.0 copy-done
  152.0 0.1 copy.9
  152.2 0.8 copy.12
  153.0 0.1 copy.10
  153.2 0.8 copy.13
  (2 shorter events, 0.1 us)
Async XLA Ops:
  149.0 2.9 %copy-start = (bf16[4,2,128,128]{3,2,1,0:T(8,128)(2,1)S(1)}, bf16[4,2,128,128]{3,2,1,0:T(8,128)(2,1)}, u32[]{:S(2)}) copy-start(bf16[4,2,128,128]{3,2,1,0:T(8,128)(2,1)} %get-tuple-element.9) | copy-start | bytes 786436

commit v2 on v1

--- a/solution.py
+++ b/solution.py
@@ -31,17 +31,18 @@
 
 
 def kernel(
-    G, NB, SH, T, D,
+    G, NB, NH, SH, T, D,
     w_ref, q_ref, k_ref, v_ref,
-    dq_out, dkv_out, loss_out,
-    qs, kvs, kts, vts, o_near, o_far, stats, dos, dqs, dkv_acc, dkv_send, dkv_recv, dkv_fin, loss_acc,
+    dq_out, dk_out, dv_out, loss_out,
+    qs, kvs, kts, vts, o_near, o_far, stats, dos, dqs, dkv_acc, dkv_send, dkv_recv, dkv_fin, loss_acc, l_head, l_group, l_line,
     q_send, q_recv, k_send, k_recv, v_send, v_recv, kv_send, kv_recv,
-    g_send, g_recv, dq_send, dq_recv, f_send, f_recv, loc,
+    g_send, g_recv, dq_send, dq_recv, f_send, f_recv, e_send, e_recv, lh_send, lh_recv, lg_send, lg_recv, ll_send, ll_recv, loc,
 ):
     R = G * SH
     NT = R // T
     QW = GS * HD
     me = lax.axis_index("ctx")
+    hd = lax.axis_index("head")
     z = me // G
     p = lax.rem(me, G)
     c = math.log2(math.e) / math.sqrt(HD)
@@ -59,7 +60,9 @@
         return carry
 
     lax.fori_loop(1, NB, greet, 0)
-    pl.semaphore_wait(barrier, G - 1 + NB - 1)
+    for o in range(1, NH):
+        pl.semaphore_signal(barrier, inc=1, device_id={"head": lax.rem(hd + o, NH)}, device_id_type=MESH)
+    pl.semaphore_wait(barrier, G - 1 + NB - 1 + NH - 1)
 
     def my_rows(pp):
         return pl.ds(pl.multiple_of(pp * SH, SH), SH)
@@ -270,7 +273,44 @@
 
     for rt in range(NT):
         heads(lambda h: middle(h, rt))
-    loss_out[...] = loss_acc[...]
+    head_loss = loss_acc[:, 0:128]
+    for lane in range(128, T, 128):
+        head_loss = head_loss + loss_acc[:, lane:lane + 128]
+    l_head[hd] = head_loss
+
+    def loss_copies(buf, count, mine, send, recv, where):
+        def one(o, carry, act):
+            to = lax.rem(mine + o, count)
+            act(pltpu.make_async_remote_copy(
+                src_ref=buf.at[mine], dst_ref=buf.at[mine],
+                send_sem=send.at[to], recv_sem=recv.at[mine],
+                device_id=where(to), device_id_type=MESH))
+            return carry
+
+        def got(o, carry):
+            frm = lax.rem(mine + o, count)
+            pltpu.make_async_remote_copy(
+                src_ref=buf.at[frm], dst_ref=buf.at[frm],
+                send_sem=send.at[frm], recv_sem=recv.at[frm],
+                device_id=where(frm), device_id_type=MESH).wait_recv()
+            return carry
+
+        def start():
+            lax.fori_loop(1, count, functools.partial(one, act=lambda x: x.start()), 0)
+
+        def total():
+            lax.fori_loop(1, count, got, 0)
+            return lax.fori_loop(1, count, lambda i, t: t + buf[i], buf[0])
+
+        def drain():
+            lax.fori_loop(1, count, functools.partial(one, act=lambda x: x.wait_send()), 0)
+
+        return start, total, drain
+
+    loss_head = loss_copies(l_head, NH, hd, lh_send, lh_recv, lambda to: {"head": to})
+    loss_group = loss_copies(l_group, G, p, lg_send, lg_recv, lambda to: dev(z, to))
+    loss_line = loss_copies(l_line, NB, z, ll_send, ll_recv, lambda to: dev(to, p))
+    loss_head[0]()
 
     def backward(h, d, rt, block):
         rows = slice(rt * T, (rt + 1) * T)
@@ -307,21 +347,24 @@
 
     def dq_copy(to):
         return pltpu.make_async_remote_copy(
-            src_ref=dqs.at[my_rows(to), :], dst_ref=dq_out.at[p],
+            src_ref=dqs.at[my_rows(to), :], dst_ref=dq_out.at[:, wide(p)],
             send_sem=dq_send.at[to], recv_sem=dq_recv.at[p],
             device_id=dev(z, to), device_id_type=MESH)
 
     def dq_local(to):
-        return pltpu.make_async_copy(dqs.at[my_rows(to), :], dq_out.at[p], loc.at[2])
-
-    def fin_copy(to):
-        return pltpu.make_async_remote_copy(
-            src_ref=dkv_fin.at[:, my_rows(to), :], dst_ref=dkv_out.at[p],
-            send_sem=f_send.at[to], recv_sem=f_recv.at[p],
+        return pltpu.make_async_copy(dqs.at[my_rows(to), :], dq_out.at[:, wide(p)], loc.at[2])
+
+    def fin_copy(to, part):
+        out, send, recv = ((dk_out, f_send, f_recv), (dv_out, e_send, e_recv))[part]
+        return pltpu.make_async_remote_copy(
+            src_ref=dkv_fin.at[part, my_rows(to), :], dst_ref=out.at[:, narrow(p)],
+            send_sem=send.at[to], recv_sem=recv.at[p],
             device_id=dev(z, to), device_id_type=MESH)
 
-    def fin_local(to):
-        return pltpu.make_async_copy(dkv_fin.at[:, my_rows(to), :], dkv_out.at[p], loc.at[3])
+    def fin_local(to, part):
+        out = (dk_out, dv_out)[part]
+        return pltpu.make_async_copy(
+            dkv_fin.at[part, my_rows(to), :], out.at[:, narrow(p)], loc.at[part])
 
     for d in range(min(D, NB - 1), 0, -1):
         @pl.when(z >= d)
@@ -336,10 +379,15 @@
             dkv_send[d - 1, 1] = dkv_acc[1].astype(BF16)
             term_copy(d, z - d).start()
 
+    l_group[p] = loss_head[1]()
+    loss_group[0]()
     dkv_acc[...] = jnp.zeros_like(dkv_acc)
     turn(kts, z, 0)
     for rt in range(NT):
         heads(lambda h: backward(h, 0, rt, z))
+        if rt == 0:
+            l_line[z] = loss_group[1]()
+            loss_line[0]()
         for to in range(rt * T // SH, (rt + 1) * T // SH):
             @pl.when(p != to)
             def _():
@@ -359,11 +407,13 @@
     for to in range(G):
         @pl.when(p != to)
         def _():
-            fin_copy(to).start()
+            fin_copy(to, 0).start()
+            fin_copy(to, 1).start()
 
         @pl.when(p == to)
         def _():
-            fin_local(to).start()
+            fin_local(to, 0).start()
+            fin_local(to, 1).start()
 
     def drain_up(to_z, carry):
         block_copy(z, to_z).wait_send()
@@ -379,18 +429,24 @@
         def _():
             term_copy(d, z - d).wait_send()
     dq_local(p).wait()
-    fin_local(p).wait()
+    fin_local(p, 0).wait()
+    fin_local(p, 1).wait()
+    loss_out[0, 0] = jnp.sum(loss_line[1]()) / (NB * R * QH * HD)
+    for part in (loss_head, loss_group, loss_line):
+        part[2]()
     for o in range(1, G):
         other = lax.rem(p + o, G)
         dq_copy(other).wait_send()
-        fin_copy(other).wait_send()
+        for part in range(2):
+            fin_copy(other, part).wait_send()
+            out, send, recv = ((dk_out, f_send, f_recv), (dv_out, e_send, e_recv))[part]
+            landed = out.at[:, narrow(other)]
+            pltpu.make_async_remote_copy(
+                src_ref=landed, dst_ref=landed, send_sem=send.at[other], recv_sem=recv.at[other],
+                device_id=dev(z, other), device_id_type=MESH).wait_recv()
+        landed = dq_out.at[:, wide(other)]
         pltpu.make_async_remote_copy(
-            src_ref=dq_out.at[other], dst_ref=dq_out.at[other],
-            send_sem=dq_send.at[other], recv_sem=dq_recv.at[other],
-            device_id=dev(z, other), device_id_type=MESH).wait_recv()
-        pltpu.make_async_remote_copy(
-            src_ref=dkv_out.at[other], dst_ref=dkv_out.at[other],
-            send_sem=f_send.at[other], recv_sem=f_recv.at[other],
+            src_ref=landed, dst_ref=landed, send_sem=dq_send.at[other], recv_sem=dq_recv.at[other],
             device_id=dev(z, other), device_id_type=MESH).wait_recv()
 
 
@@ -405,15 +461,17 @@
     DS = max(1, min(D, NB - 1))
     dma = pltpu.SemaphoreType.DMA
     any_spec = pl.BlockSpec(memory_space=pl.ANY)
-    dq, dkv, loss_part = pl.pallas_call(
-        functools.partial(kernel, G, NB, sh, T, D),
+    NH = lax.axis_size("head")
+    dq, dk, dv, loss = pl.pallas_call(
+        functools.partial(kernel, G, NB, NH, sh, T, D),
         out_shape=(
-            jax.ShapeDtypeStruct((G, sh, GS * HD), BF16),
-            jax.ShapeDtypeStruct((G, 2, sh, HD), BF16),
-            jax.ShapeDtypeStruct((8, T), F32),
+            jax.ShapeDtypeStruct((sh, G * GS * HD), BF16),
+            jax.ShapeDtypeStruct((sh, G * HD), BF16),
+            jax.ShapeDtypeStruct((sh, G * HD), BF16),
+            jax.ShapeDtypeStruct((1, 1), F32),
         ),
         in_specs=[pl.BlockSpec(memory_space=pltpu.SMEM), any_spec, any_spec, any_spec],
-        out_specs=(any_spec, any_spec, pl.BlockSpec(memory_space=pltpu.VMEM)),
+        out_specs=(any_spec, any_spec, any_spec, pl.BlockSpec(memory_space=pltpu.SMEM)),
         scratch_shapes=[
             pltpu.VMEM((R, GS * HD), BF16),
             pltpu.VMEM((NB, 2, R, HD), BF16),
@@ -429,19 +487,20 @@
             pltpu.VMEM((DS, 2, R, HD), BF16),
             pltpu.VMEM((2, R, HD), BF16),
             pltpu.VMEM((8, T), F32),
+            pltpu.VMEM((NH, 8, 128), F32),
+            pltpu.VMEM((G, 8, 128), F32),
+            pltpu.VMEM((NB, 8, 128), F32),
             dma((G,)), dma((G,)), dma((G,)), dma((G,)), dma((G,)), dma((G,)),
             dma((NB,)), dma((NB,)),
             dma((DS,)), dma((DS,)),
-            dma((G,)), dma((G,)), dma((G,)), dma((G,)),
+            dma((G,)), dma((G,)), dma((G,)), dma((G,)), dma((G,)), dma((G,)),
+            dma((NH,)), dma((NH,)), dma((G,)), dma((G,)), dma((NB,)), dma((NB,)),
             dma((4,)),
         ],
         compiler_params=pltpu.CompilerParams(
             collective_id=0, has_side_effects=True, vmem_limit_bytes=56 * 1024 * 1024),
     )(window, queries, keys, values)
-    loss = lax.psum(jnp.sum(loss_part), ("ctx", "head")) / (sh * n_ctx * QH * HD)
-    grad_q = dq.transpose(1, 0, 2).reshape(sh, -1).astype(F32)
-    grads = dkv.transpose(1, 2, 0, 3).reshape(2, sh, -1).astype(F32)
-    return (loss, grad_q, grads[0], grads[1])
+    return (loss[0, 0], dq.astype(F32), dk.astype(F32), dv.astype(F32))
 
 
 def solution(mesh):

time: 158 us -> 112 us (0.71); the launches traced: 155 us -> 112 us
  blocking collectives: 38.3 us -> 0 us
  local copies, waits for them, and re-layouts: 6.76 us -> 0.01 us
    psum x1 -> x0, blocking collectives: 38.3 us -> none  [body(): lax.psum(jnp.sum(loss_part), ('ctx', 'head')) / (sh * n_ctx * QH * HD)]
    unnamed x5 -> x4, local copies, waits for them, and re-layouts: 4.6 us -> 0.01 us
    convert_element_type x2 -> x3, other arithmetic: 1.5 us -> 4.26 us  [body(): return (loss[0, 0], dq.astype(F32), dk.astype(F32), dv.astype(F32))]
    convert_element_type x1 -> x0, local copies, waits for them, and re-layouts: 1.87 us -> none  [body(): grad_q = dq.transpose(1, 0, 2).reshape(sh, -1).astype(F32)]
where the time goes in v2:
time: 112 us
  Pallas kernels  105 us (94%)
  other arithmetic  4.26 us (4%)
  between operations  2.36 us (2%)
    pallas_call x1, Pallas kernels, body(): pl.pallas_call(functools.partial(kernel, G, NB, NH, sh, T, D), out_shape=...  105 us
    convert_element_type x3, other arithmetic, body(): return (loss[0, 0], dq.astype(F32), dk.astype(F32), dv.astype(F32))  4.26 us

profile of v2, /device:TPU:28, one launch (start us, length us, event | category | flops | bytes accessed | tf_op | source)
XLA Modules:
  0.0 111.7 jit_solution(9911075470538615402)
XLA Ops:
  0.6 105.1 %shard_map.75 = (bf16[128,4096]{1,0:T(8,128)(2,1)}, bf16[128,512]{1,0:T(8,128)(2,1)}, bf16[128,512]{1,0:T(8,128)(2,1)}, f32[1,1]{1,0:T(1,128)}) custom-call(s32[4]{0:T(128)} %w_ref.1, bf16[128,4096]{1,0:T(8,128)(2,1)} %q_ref.1, bf16[128,512]{1,0:T(8,128)(2,1)} %k_ref.1, bf16[128,512]{1,0:T(8,128)(2,1)} %v_ref.1), custom_call_target="tpu_custom_call" | custom-call | tf_op jit(solution)/shard_map/pallas_call | solution.py:465
  105.7 0.0 copy-start.1
  105.8 0.0 copy-start
  105.8 2.8 %convert_element_type.9 = f32[128,4096]{1,0:T(8,128)} convert(bf16[128,4096]{1,0:T(8,128)(2,1)} %get-tuple-element.9) | non-fusion elementwise | flops 524288 | bytes 3145728 | tf_op jit(solution)/shard_map/convert_element_type | solution.py:503
  108.6 0.0 copy-done.1
  108.6 0.7 convert_element_type.10
  109.3 0.0 copy-done
  109.3 0.7 convert_element_type.11
Async XLA Ops:
  105.7 2.8 %copy-start.1 = (bf16[128,512]{1,0:T(8,128)(2,1)S(1)}, bf16[128,512]{1,0:T(8,128)(2,1)}, u32[]{:S(2)}) copy-start(bf16[128,512]{1,0:T(8,128)(2,1)} %get-tuple-element.10) | copy-start | bytes 393220
  105.8 3.5 %copy-start = (bf16[128,512]{1,0:T(8,128)(2,1)S(1)}, bf16[128,512]{1,0:T(8,128)(2,1)}, u32[]{:S(2)}) copy-start(bf16[128,512]{1,0:T(8,128)(2,1)} %get-tuple-element.11) | copy-start | bytes 393220

commit v3 on v2

--- a/solution.py
+++ b/solution.py
@@ -14,6 +14,8 @@
 WIN_MAX = 1024
 WIN_MIN = 512
 GS = QH // KVH
+FWD_HEADS = 4
+BWD_HEADS = 4
 
 MESH = pl.DeviceIdType.MESH
 NEG = -1e30
@@ -167,6 +169,7 @@
         for kt, delta, near, far in ([(kt, None, False, True) for kt in range(NT)] if far_only else tiles_of(d, rt)):
             keys = kvs[block, 0, kt * T:(kt + 1) * T, :]
             work.append((kt, delta, near, far, dot_nt(keys, q) * c))
+        yield
         has_near = any(t[2] for t in work)
         has_far = any(t[3] for t in work)
         if has_near:
@@ -193,6 +196,7 @@
                 new_s = top if new_s is None else jnp.maximum(new_s, top)
             if far:
                 new_f = jnp.maximum(new_f, jnp.max(s_far, axis=0, keepdims=True))
+        yield
         near_sum, far_sum, near_o, far_o = 0.0, 0.0, 0.0, 0.0
         for (kt, delta, near, far, s), mask in zip(work, masks):
             vt = vts[:, kt * T:(kt + 1) * T]
@@ -210,6 +214,7 @@
             if far:
                 far_sum = far_sum + jnp.sum(p_far, axis=0, keepdims=True)
                 far_o = far_o + dot_nn(vt, p_far.astype(BF16))
+        yield
         if has_near:
             if d == 0:
                 stats[h, 1:2, rows] = near_sum
@@ -225,11 +230,25 @@
             o_far[h, :, rows] = o_far[h, :, rows] * factor + far_o
             stats[h, 2:3, rows] = new_f
 
-    def heads(fn):
-        def step(h, carry):
-            fn(h)
+    def heads(fn, count=1, finish=None):
+        def step(i, carry):
+            running = [fn(i * count + j) for j in range(count)]
+            if running[0] is not None:
+                totals = []
+                while running:
+                    alive = []
+                    for one in running:
+                        try:
+                            next(one)
+                            alive.append(one)
+                        except StopIteration as end:
+                            if end.value is not None:
+                                totals.append(end.value)
+                    running = alive
+                if finish is not None:
+                    finish(totals)
             return carry
-        lax.fori_loop(0, GS, step, 0)
+        lax.fori_loop(0, GS // count, step, 0)
 
     def arrive(block):
         block_copy(block, z).wait_recv()
@@ -242,7 +261,7 @@
                 arrive(block)
             turn(vts, block, 1)
             for rt in range(NT):
-                heads(lambda h: forward(h, d, rt, block))
+                heads(lambda h: forward(h, d, rt, block), FWD_HEADS)
 
     if NB - 1 > D:
         def far_block(d, carry):
@@ -250,7 +269,7 @@
             arrive(block)
             turn(vts, block, 1)
             for rt in range(NT):
-                heads(lambda h: forward(h, None, rt, block, True))
+                heads(lambda h: forward(h, None, rt, block, True), FWD_HEADS)
             return carry
         lax.fori_loop(D + 1, z + 1, far_block, 0)
 
@@ -319,25 +338,37 @@
         lse = stats[h, 4:5, rows]
         rd = stats[h, 5:6, rows]
         dq = o_near[h, :, rows]
+        work = []
         for kt, delta, near, far in tiles_of(d, rt):
-            if not near:
-                continue
-            part = slice(kt * T, (kt + 1) * T)
-            s = dot_nt(kvs[block, 0, part, :], q) * c
+            if near:
+                part = slice(kt * T, (kt + 1) * T)
+                work.append((part, delta, far, dot_nt(kvs[block, 0, part, :], q) * c,
+                             dot_nt(kvs[block, 1, part, :], do)))
+        yield
+        terms = []
+        for part, delta, far, s, dp in work:
             if far:
                 s = jnp.where(ramp < window - delta, s, NEG)
             elif delta == 0:
                 s = jnp.where(ramp >= 0, s, NEG)
             w = jnp.exp2(s - lse)
-            dp = dot_nt(kvs[block, 1, part, :], do)
             ds = (w * (dp - rd)).astype(BF16)
-            dkv_acc[1, part, :] += dot_nn(w.astype(BF16), do)
-            dkv_acc[0, part, :] += dot_nn(ds, q)
+            dv = dot_nn(w.astype(BF16), do)
+            dk = dot_nn(ds, q)
             dq = dq + dot_nn(kts[:, part], ds)
+            terms.append((part, dk, dv))
+        yield
         if d == 0:
             dqs[rows, narrow(h)] = (dq * inv_root).T.astype(BF16)
         else:
             o_near[h, :, rows] = dq
+        return terms
+
+    def add_terms(per_head):
+        for same in zip(*per_head):
+            part = same[0][0]
+            dkv_acc[0, part, :] += sum(t[1] for t in same)
+            dkv_acc[1, part, :] += sum(t[2] for t in same)
 
     def term_copy(d, to_z):
         return pltpu.make_async_remote_copy(
@@ -374,7 +405,7 @@
             turn(kts, block, 0)
             for rt in range(NT):
                 if any(t[2] for t in tiles_of(d, rt)):
-                    heads(lambda h: backward(h, d, rt, block))
+                    heads(lambda h: backward(h, d, rt, block), BWD_HEADS, add_terms)
             dkv_send[d - 1, 0] = (dkv_acc[0] * inv_root).astype(BF16)
             dkv_send[d - 1, 1] = dkv_acc[1].astype(BF16)
             term_copy(d, z - d).start()
@@ -384,7 +415,7 @@
     dkv_acc[...] = jnp.zeros_like(dkv_acc)
     turn(kts, z, 0)
     for rt in range(NT):
-        heads(lambda h: backward(h, 0, rt, z))
+        heads(lambda h: backward(h, 0, rt, z), BWD_HEADS, add_terms)
         if rt == 0:
             l_line[z] = loss_group[1]()
             loss_line[0]()

time: 112 us -> 81.4 us (0.73)
  Pallas kernels: 105 us -> 74.6 us
    pallas_call x1, Pallas kernels: 105 us -> 74.6 us  [body(): pl.pallas_call(functools.partial(kernel, G, NB, NH, sh, T, D), out_shape=...]
where the time goes in v3:
time: 81.4 us; the launch traced here: 81.2 us
  Pallas kernels  74.6 us (92%)
  other arithmetic  4.26 us (5%)
  between operations  2.36 us (3%)
    pallas_call x1, Pallas kernels, body(): pl.pallas_call(functools.partial(kernel, G, NB, NH, sh, T, D), out_shape=...  74.6 us
    convert_element_type x3, other arithmetic, body(): return (loss[0, 0], dq.astype(F32), dk.astype(F32), dv.astype(F32))  4.26 us

profile of v3, /device:TPU:28, one launch (start us, length us, event | category | flops | bytes accessed | tf_op | source)
XLA Modules:
  0.0 81.2 jit_solution(10335150823081447307)
XLA Ops:
  0.6 74.6 %shard_map.75 = (bf16[128,4096]{1,0:T(8,128)(2,1)}, bf16[128,512]{1,0:T(8,128)(2,1)}, bf16[128,512]{1,0:T(8,128)(2,1)}, f32[1,1]{1,0:T(1,128)}) custom-call(s32[4]{0:T(128)} %w_ref.1, bf16[128,4096]{1,0:T(8,128)(2,1)} %q_ref.1, bf16[128,512]{1,0:T(8,128)(2,1)} %k_ref.1, bf16[128,512]{1,0:T(8,128)(2,1)} %v_ref.1), custom_call_target="tpu_custom_call" | custom-call | tf_op jit(solution)/shard_map/pallas_call | solution.py:496
  75.2 0.0 copy-start.1
  75.2 0.0 copy-start
  75.2 2.8 %convert_element_type.9 = f32[128,4096]{1,0:T(8,128)} convert(bf16[128,4096]{1,0:T(8,128)(2,1)} %get-tuple-element.9) | non-fusion elementwise | flops 524288 | bytes 3145728 | tf_op jit(solution)/shard_map/convert_element_type | solution.py:534
  78.0 0.0 copy-done.1
  78.0 0.7 convert_element_type.10
  78.7 0.0 copy-done
  78.7 0.7 convert_element_type.11
Async XLA Ops:
  75.2 2.8 %copy-start.1 = (bf16[128,512]{1,0:T(8,128)(2,1)S(1)}, bf16[128,512]{1,0:T(8,128)(2,1)}, u32[]{:S(2)}) copy-start(bf16[128,512]{1,0:T(8,128)(2,1)} %get-tuple-element.10) | copy-start | bytes 393220
  75.2 3.5 %copy-start = (bf16[128,512]{1,0:T(8,128)(2,1)S(1)}, bf16[128,512]{1,0:T(8,128)(2,1)}, u32[]{:S(2)}) copy-start(bf16[128,512]{1,0:T(8,128)(2,1)} %get-tuple-element.11) | copy-start | bytes 393220

commit v4 on v3

--- a/solution.py
+++ b/solution.py
@@ -16,6 +16,7 @@
 GS = QH // KVH
 FWD_HEADS = 4
 BWD_HEADS = 4
+PARTS = 2
 
 MESH = pl.DeviceIdType.MESH
 NEG = -1e30
@@ -83,12 +84,18 @@
             send_sem=send.at[to], recv_sem=recv.at[p],
             device_id=dev(z, to), device_id_type=MESH)
 
-    def q_copy(o):
+    PW = QW // PARTS
+    PH = GS // PARTS
+
+    def part_of(pp, part):
+        return pl.ds(pl.multiple_of(pp * QW + part * PW, PW), PW)
+
+    def q_copy(o, part):
         to = lax.rem(p + o, G)
         return pltpu.make_async_remote_copy(
-            src_ref=q_ref.at[:, wide(to)],
-            dst_ref=qs.at[my_rows(p), :],
-            send_sem=q_send.at[to], recv_sem=q_recv.at[p],
+            src_ref=q_ref.at[:, part_of(to, part)],
+            dst_ref=qs.at[my_rows(p), part_of(0, part)],
+            send_sem=q_send.at[part, to], recv_sem=q_recv.at[part, p],
             device_id=dev(z, to), device_id_type=MESH)
 
     def recv_kv(frm, part, recv):
@@ -100,8 +107,9 @@
     for o in range(1, G):
         kv_copy(k_ref, 0, o, k_send, k_recv).start()
         kv_copy(v_ref, 1, o, v_send, v_recv).start()
-    for o in range(1, G):
-        q_copy(o).start()
+    for part in range(PARTS):
+        for o in range(1, G):
+            q_copy(o, part).start()
     local = [
         pltpu.make_async_copy(k_ref.at[:, narrow(p)], kvs.at[z, 0, my_rows(p), :], loc.at[0]),
         pltpu.make_async_copy(v_ref.at[:, narrow(p)], kvs.at[z, 1, my_rows(p), :], loc.at[1]),
@@ -138,12 +146,15 @@
         return carry
 
     lax.fori_loop(z + 1, NB, send_up, 0)
-    for o in range(1, G):
-        frm = lax.rem(p + o, G)
-        pltpu.make_async_remote_copy(
-            src_ref=qs.at[my_rows(frm), :], dst_ref=qs.at[my_rows(frm), :],
-            send_sem=q_send.at[frm], recv_sem=q_recv.at[frm],
-            device_id=dev(z, frm), device_id_type=MESH).wait_recv()
+
+    def q_arrive(part):
+        for o in range(1, G):
+            frm = lax.rem(p + o, G)
+            landed = qs.at[my_rows(frm), part_of(0, part)]
+            pltpu.make_async_remote_copy(
+                src_ref=landed, dst_ref=landed,
+                send_sem=q_send.at[part, frm], recv_sem=q_recv.at[part, frm],
+                device_id=dev(z, frm), device_id_type=MESH).wait_recv()
 
     window = w_ref[p]
     ramp = lax.broadcasted_iota(jnp.int32, (T, T), 1) - lax.broadcasted_iota(jnp.int32, (T, T), 0)
@@ -230,7 +241,7 @@
             o_far[h, :, rows] = o_far[h, :, rows] * factor + far_o
             stats[h, 2:3, rows] = new_f
 
-    def heads(fn, count=1, finish=None):
+    def heads(fn, count=1, finish=None, low=0, high=GS):
         def step(i, carry):
             running = [fn(i * count + j) for j in range(count)]
             if running[0] is not None:
@@ -248,7 +259,7 @@
                 if finish is not None:
                     finish(totals)
             return carry
-        lax.fori_loop(0, GS // count, step, 0)
+        lax.fori_loop(low // count, high // count, step, 0)
 
     def arrive(block):
         block_copy(block, z).wait_recv()
@@ -259,9 +270,16 @@
             block = z - d
             if d > 0:
                 arrive(block)
-            turn(vts, block, 1)
-            for rt in range(NT):
-                heads(lambda h: forward(h, d, rt, block), FWD_HEADS)
+                turn(vts, block, 1)
+                for rt in range(NT):
+                    heads(lambda h: forward(h, d, rt, block), FWD_HEADS)
+            else:
+                turn(vts, block, 1)
+                turn(kts.at[0], block, 0)
+                for part in range(PARTS):
+                    q_arrive(part)
+                    for rt in range(NT):
+                        heads(lambda h: forward(h, d, rt, block), FWD_HEADS, None, part * PH, part * PH + PH)
 
     if NB - 1 > D:
         def far_block(d, carry):
@@ -281,17 +299,19 @@
         a_s, a_f = jnp.exp2(m_s - m_t), jnp.exp2(m_f - m_t)
         total = l_s * a_s + l_f * a_f
         near = o_near[h, :, rows]
-        student = near / l_s
-        teacher = (near * a_s + o_far[h, :, rows] * a_f) / total
+        student = near * (1.0 / l_s)
+        teacher = near * (a_s / total) + o_far[h, :, rows] * (a_f / total)
         diff = student - teacher.astype(BF16).astype(F32)
-        loss_acc[...] += jnp.sum((diff * diff).reshape(HD // 8, 8, T), axis=0)
+        squares = jnp.sum((diff * diff).reshape(HD // 8, 8, T), axis=0)
+        yield
+        loss_acc[...] += squares
         stats[h, 4:5, rows] = m_s + jnp.log2(l_s)
         stats[h, 5:6, rows] = jnp.sum(diff * student, axis=0, keepdims=True)
         dos[rows, narrow(h)] = diff.T.astype(BF16)
         o_near[h, :, rows] = jnp.zeros((HD, T), F32)
 
     for rt in range(NT):
-        heads(lambda h: middle(h, rt))
+        heads(lambda h: middle(h, rt), FWD_HEADS)
     head_loss = loss_acc[:, 0:128]
     for lane in range(128, T, 128):
         head_loss = head_loss + loss_acc[:, lane:lane + 128]
@@ -355,8 +375,8 @@
             ds = (w * (dp - rd)).astype(BF16)
             dv = dot_nn(w.astype(BF16), do)
             dk = dot_nn(ds, q)
-            dq = dq + dot_nn(kts[:, part], ds)
-            terms.append((part, dk, dv))
+            dq = dq + dot_nn(kts[min(d, 1), :, part], ds)
+            terms.append((dkv_acc.at[min(d, 1)], part, dk, dv))
         yield
         if d == 0:
             dqs[rows, narrow(h)] = (dq * inv_root).T.astype(BF16)
@@ -366,9 +386,9 @@
 
     def add_terms(per_head):
         for same in zip(*per_head):
-            part = same[0][0]
-            dkv_acc[0, part, :] += sum(t[1] for t in same)
-            dkv_acc[1, part, :] += sum(t[2] for t in same)
+            acc, part = same[0][:2]
+            acc[0, part, :] += sum(t[2] for t in same)
+            acc[1, part, :] += sum(t[3] for t in same)
 
     def term_copy(d, to_z):
         return pltpu.make_async_remote_copy(
@@ -376,14 +396,15 @@
             send_sem=g_send.at[d - 1], recv_sem=g_recv.at[d - 1],
             device_id=dev(to_z, p), device_id_type=MESH)
 
-    def dq_copy(to):
-        return pltpu.make_async_remote_copy(
-            src_ref=dqs.at[my_rows(to), :], dst_ref=dq_out.at[:, wide(p)],
-            send_sem=dq_send.at[to], recv_sem=dq_recv.at[p],
+    def dq_copy(to, part):
+        return pltpu.make_async_remote_copy(
+            src_ref=dqs.at[my_rows(to), part_of(0, part)], dst_ref=dq_out.at[:, part_of(p, part)],
+            send_sem=dq_send.at[part, to], recv_sem=dq_recv.at[part, p],
             device_id=dev(z, to), device_id_type=MESH)
 
-    def dq_local(to):
-        return pltpu.make_async_copy(dqs.at[my_rows(to), :], dq_out.at[:, wide(p)], loc.at[2])
+    def dq_local(to, part):
+        return pltpu.make_async_copy(
+            dqs.at[my_rows(to), part_of(0, part)], dq_out.at[:, part_of(p, part)], loc.at[2 + part])
 
     def fin_copy(to, part):
         out, send, recv = ((dk_out, f_send, f_recv), (dv_out, e_send, e_recv))[part]
@@ -397,44 +418,54 @@
         return pltpu.make_async_copy(
             dkv_fin.at[part, my_rows(to), :], out.at[:, narrow(p)], loc.at[part])
 
-    for d in range(min(D, NB - 1), 0, -1):
+    def back(d, part):
+        for rt in range(NT):
+            if any(t[2] for t in tiles_of(d, rt)):
+                if part is None:
+                    heads(lambda h: backward(h, d, rt, z - d), BWD_HEADS, add_terms)
+                else:
+                    heads(lambda h: backward(h, d, rt, z - d), BWD_HEADS, add_terms, part * PH, part * PH + PH)
+
+    def send_term(d):
+        dkv_send[d - 1, 0] = (dkv_acc[1, 0] * inv_root).astype(BF16)
+        dkv_send[d - 1, 1] = dkv_acc[1, 1].astype(BF16)
+        term_copy(d, z - d).start()
+
+    top = min(D, NB - 1)
+    dkv_acc[0] = jnp.zeros(dkv_acc.shape[1:], F32)
+    for d in range(top, 0, -1):
         @pl.when(z >= d)
         def _():
-            block = z - d
-            dkv_acc[...] = jnp.zeros_like(dkv_acc)
-            turn(kts, block, 0)
-            for rt in range(NT):
-                if any(t[2] for t in tiles_of(d, rt)):
-                    heads(lambda h: backward(h, d, rt, block), BWD_HEADS, add_terms)
-            dkv_send[d - 1, 0] = (dkv_acc[0] * inv_root).astype(BF16)
-            dkv_send[d - 1, 1] = dkv_acc[1].astype(BF16)
-            term_copy(d, z - d).start()
+            dkv_acc[1] = jnp.zeros(dkv_acc.shape[1:], F32)
+            turn(kts.at[1], z - d, 0)
+            if d > 1:
+                back(d, None)
+                send_term(d)
 
     l_group[p] = loss_head[1]()
     loss_group[0]()
-    dkv_acc[...] = jnp.zeros_like(dkv_acc)
-    turn(kts, z, 0)
-    for rt in range(NT):
-        heads(lambda h: backward(h, 0, rt, z), BWD_HEADS, add_terms)
-        if rt == 0:
+    for part in range(PARTS):
+        if top > 0:
+            @pl.when(z >= 1)
+            def _():
+                back(1, part)
+                if part == PARTS - 1:
+                    send_term(1)
+        back(0, part)
+        if part == 0:
             l_line[z] = loss_group[1]()
             loss_line[0]()
-        for to in range(rt * T // SH, (rt + 1) * T // SH):
-            @pl.when(p != to)
-            def _():
-                dq_copy(to).start()
-
-            @pl.when(p == to)
-            def _():
-                dq_local(to).start()
-
-    dkv_acc[0] = dkv_acc[0] * inv_root
-    for d in range(1, min(D, NB - 1) + 1):
+        for o in range(1, G):
+            dq_copy(lax.rem(p + o, G), part).start()
+        dq_local(p, part).start()
+
+    dkv_acc[0, 0] = dkv_acc[0, 0] * inv_root
+    for d in range(top, 0, -1):
         @pl.when(z + d < NB)
         def _():
             term_copy(d, z).wait_recv()
-            dkv_acc[...] += dkv_recv[d - 1].astype(F32)
-    dkv_fin[...] = dkv_acc[...].astype(BF16)
+            dkv_acc[0] += dkv_recv[d - 1].astype(F32)
+    dkv_fin[...] = dkv_acc[0].astype(BF16)
     for to in range(G):
         @pl.when(p != to)
         def _():
@@ -453,13 +484,15 @@
     for o in range(1, G):
         kv_copy(k_ref, 0, o, k_send, k_recv).wait_send()
         kv_copy(v_ref, 1, o, v_send, v_recv).wait_send()
-        q_copy(o).wait_send()
+        for part in range(PARTS):
+            q_copy(o, part).wait_send()
     lax.fori_loop(z + 1, NB, drain_up, 0)
     for d in range(1, min(D, NB - 1) + 1):
         @pl.when(z >= d)
         def _():
             term_copy(d, z - d).wait_send()
-    dq_local(p).wait()
+    for part in range(PARTS):
+        dq_local(p, part).wait()
     fin_local(p, 0).wait()
     fin_local(p, 1).wait()
     loss_out[0, 0] = jnp.sum(loss_line[1]()) / (NB * R * QH * HD)
@@ -467,7 +500,13 @@
         part[2]()
     for o in range(1, G):
         other = lax.rem(p + o, G)
-        dq_copy(other).wait_send()
+        for part in range(PARTS):
+            dq_copy(other, part).wait_send()
+            landed = dq_out.at[:, part_of(other, part)]
+            pltpu.make_async_remote_copy(
+                src_ref=landed, dst_ref=landed,
+                send_sem=dq_send.at[part, other], recv_sem=dq_recv.at[part, other],
+                device_id=dev(z, other), device_id_type=MESH).wait_recv()
         for part in range(2):
             fin_copy(other, part).wait_send()
             out, send, recv = ((dk_out, f_send, f_recv), (dv_out, e_send, e_recv))[part]
@@ -475,10 +514,6 @@
             pltpu.make_async_remote_copy(
                 src_ref=landed, dst_ref=landed, send_sem=send.at[other], recv_sem=recv.at[other],
                 device_id=dev(z, other), device_id_type=MESH).wait_recv()
-        landed = dq_out.at[:, wide(other)]
-        pltpu.make_async_remote_copy(
-            src_ref=landed, dst_ref=landed, send_sem=dq_send.at[other], recv_sem=dq_recv.at[other],
-            device_id=dev(z, other), device_id_type=MESH).wait_recv()
 
 
 def body(queries, keys, values, window):
@@ -506,14 +541,14 @@
         scratch_shapes=[
             pltpu.VMEM((R, GS * HD), BF16),
             pltpu.VMEM((NB, 2, R, HD), BF16),
-            pltpu.VMEM((HD, R), BF16),
+            pltpu.VMEM((2, HD, R), BF16),
             pltpu.VMEM((HD, R), BF16),
             pltpu.VMEM((GS, HD, R), F32),
             pltpu.VMEM((GS, HD, R), F32),
             pltpu.VMEM((GS, 8, R), F32),
             pltpu.VMEM((R, GS * HD), BF16),
             pltpu.VMEM((R, GS * HD), BF16),
-            pltpu.VMEM((2, R, HD), F32),
+            pltpu.VMEM((2, 2, R, HD), F32),
             pltpu.VMEM((DS, 2, R, HD), BF16),
             pltpu.VMEM((DS, 2, R, HD), BF16),
             pltpu.VMEM((2, R, HD), BF16),
@@ -521,12 +556,12 @@
             pltpu.VMEM((NH, 8, 128), F32),
             pltpu.VMEM((G, 8, 128), F32),
             pltpu.VMEM((NB, 8, 128), F32),
-            dma((G,)), dma((G,)), dma((G,)), dma((G,)), dma((G,)), dma((G,)),
+            dma((PARTS, G)), dma((PARTS, G)), dma((G,)), dma((G,)), dma((G,)), dma((G,)),
             dma((NB,)), dma((NB,)),
             dma((DS,)), dma((DS,)),
-            dma((G,)), dma((G,)), dma((G,)), dma((G,)), dma((G,)), dma((G,)),
+            dma((PARTS, G)), dma((PARTS, G)), dma((G,)), dma((G,)), dma((G,)), dma((G,)),
             dma((NH,)), dma((NH,)), dma((G,)), dma((G,)), dma((NB,)), dma((NB,)),
-            dma((4,)),
+            dma((2 + PARTS,)),
         ],
         compiler_params=pltpu.CompilerParams(
             collective_id=0, has_side_effects=True, vmem_limit_bytes=56 * 1024 * 1024),

time: 81.4 us -> 76.1 us (0.935)
  Pallas kernels: 74.6 us -> 69.1 us
    pallas_call x1, Pallas kernels: 74.6 us -> 69.1 us  [body(): pl.pallas_call(functools.partial(kernel, G, NB, NH, sh, T, D), out_shape=...]
where the time goes in v4:
time: 76.1 us; the launch traced here: 75.7 us
  Pallas kernels  69.1 us (91%)
  other arithmetic  4.26 us (6%)
  between operations  2.36 us (3%)
    pallas_call x1, Pallas kernels, body(): pl.pallas_call(functools.partial(kernel, G, NB, NH, sh, T, D), out_shape=...  69.1 us
    convert_element_type x3, other arithmetic, body(): return (loss[0, 0], dq.astype(F32), dk.astype(F32), dv.astype(F32))  4.26 us

profile of v4, /device:TPU:28, one launch (start us, length us, event | category | flops | bytes accessed | tf_op | source)
XLA Modules:
  0.0 75.7 jit_solution(14430462113553420111)
XLA Ops:
  0.6 69.1 %shard_map.75 = (bf16[128,4096]{1,0:T(8,128)(2,1)}, bf16[128,512]{1,0:T(8,128)(2,1)}, bf16[128,512]{1,0:T(8,128)(2,1)}, f32[1,1]{1,0:T(1,128)}) custom-call(s32[4]{0:T(128)} %w_ref.1, bf16[128,4096]{1,0:T(8,128)(2,1)} %q_ref.1, bf16[128,512]{1,0:T(8,128)(2,1)} %k_ref.1, bf16[128,512]{1,0:T(8,128)(2,1)} %v_ref.1), custom_call_target="tpu_custom_call" | custom-call | tf_op jit(solution)/shard_map/pallas_call | solution.py:531
  69.7 0.0 copy-start.1
  69.7 0.0 copy-start
  69.7 2.8 %convert_element_type.9 = f32[128,4096]{1,0:T(8,128)} convert(bf16[128,4096]{1,0:T(8,128)(2,1)} %get-tuple-element.9) | non-fusion elementwise | flops 524288 | bytes 3145728 | tf_op jit(solution)/shard_map/convert_element_type | solution.py:569
  72.5 0.0 copy-done.1
  72.5 0.7 convert_element_type.10
  73.2 0.0 copy-done
  73.2 0.7 convert_element_type.11
Async XLA Ops:
  69.7 2.8 %copy-start.1 = (bf16[128,512]{1,0:T(8,128)(2,1)S(1)}, bf16[128,512]{1,0:T(8,128)(2,1)}, u32[]{:S(2)}) copy-start(bf16[128,512]{1,0:T(8,128)(2,1)} %get-tuple-element.10) | copy-start | bytes 393220
  69.7 3.5 %copy-start = (bf16[128,512]{1,0:T(8,128)(2,1)S(1)}, bf16[128,512]{1,0:T(8,128)(2,1)}, u32[]{:S(2)}) copy-start(bf16[128,512]{1,0:T(8,128)(2,1)} %get-tuple-element.11) | copy-start | bytes 393220
